TPU v7x, 32 devices: a whole 2x2x4 slice. The times are simulated.
32 devices in a mesh: tower: 2 (over core), blk: 8 (over z, x), seq: 2 (over y).
Axes of the slice: x: 2, y: 2, z: 4, core: 2. Of those that a mesh axis runs over, the one named last changes fastest.
Arguments:
- queries: bfloat16 [2, 2048, 1024], P('tower', ('blk', 'seq')), may hold values from -6 to 6
- key_rows: bfloat16 [2, 2048, 1024], P('tower', ('blk', 'seq')), may hold values from -6 to 6
- value_rows: bfloat16 [2, 2048, 1024], P('tower', ('blk', 'seq')), may hold values from -6 to 6
- cross_queries: bfloat16 [2, 2048, 1024], P('tower', ('blk', 'seq')), may hold values from -6 to 6
- cross_keys: bfloat16 [2, 2048, 1024], P('tower', ('blk', 'seq')), may hold values from -6 to 6
- cross_values: bfloat16 [2, 2048, 1024], P('tower', ('blk', 'seq')), may hold values from -6 to 6
- grad_out: bfloat16 [2, 2048, 1024], P('tower', ('blk', 'seq')), may hold values from -6 to 6
- offsets: int32 [2, 8], replicated, may hold values from -127 to 127, as said below
- key_valid: int32 [2, 2048], P(None, ('blk', 'seq')), may hold values from 0 to 1, as said below
Outputs:
- attended: bfloat16 [2, 2048, 1024], P('tower', ('blk', 'seq'))
- grad_queries: bfloat16 [2, 2048, 1024], P('tower', ('blk', 'seq'))
- grad_keys: bfloat16 [2, 2048, 1024], P('tower', ('blk', 'seq'))
- grad_values: bfloat16 [2, 2048, 1024], P('tower', ('blk', 'seq'))
- grad_cross_queries: bfloat16 [2, 2048, 1024], P('tower', ('blk', 'seq'))
- grad_cross_keys: bfloat16 [2, 2048, 1024], P('tower', ('blk', 'seq'))
- grad_cross_values: bfloat16 [2, 2048, 1024], P('tower', ('blk', 'seq'))
Inputs may be any that keep to these rules, and one draw needn't show every extreme that they name: Both ends of the range occur in every draw; for every block b, offsets[0, b] and offsets[1, b] have opposite signs, and every magnitude is at least 64. `key_valid`: positions k * 256 + 256 // 2 - 1 and k * 256 + 256 // 2 are always 1.
All inputs are finite; a program needn't handle non-finite values.
Results may differ from a plain program's by a relative error of at most 0.019.
Values may be sent and summed in bfloat16 or wider, within the bound.
A program may use at most 128 MiB of HBM per device.

v0:
```python
import functools

import jax
import jax.numpy as jnp
from jax import lax
from jax.experimental import pallas as pl
from jax.experimental.pallas import tpu as pltpu
from jax.sharding import PartitionSpec as P

HEADS = 16
HEAD = 64
WINDOW = 2048
TILE = 512
MESH = pl.DeviceIdType.MESH
F32, BF16 = jnp.float32, jnp.bfloat16


def places():
    tower, blk, seq = lax.axis_index("tower"), lax.axis_index("blk"), lax.axis_index("seq")
    peers = dict(
        y=(tower, blk, 1 - seq),
        tower=(1 - tower, blk, seq),
        diag=(1 - tower, blk, 1 - seq),
        low=(tower, blk - 1, seq),
        high=(tower, blk + 1, seq),
    )
    return tower, blk, seq, peers


def greet(blk, blks, peers):
    barrier = pltpu.get_barrier_semaphore()
    for name in ("y", "tower", "diag"):
        pl.semaphore_signal(barrier, inc=1, device_id=peers[name], device_id_type=MESH)

    @pl.when(blk > 0)
    def _():
        pl.semaphore_signal(barrier, inc=1, device_id=peers["low"], device_id_type=MESH)

    @pl.when(blk < blks - 1)
    def _():
        pl.semaphore_signal(barrier, inc=1, device_id=peers["high"], device_id_type=MESH)

    count = 3 + jnp.where(blk > 0, 1, 0) + jnp.where(blk < blks - 1, 1, 0)
    pl.semaphore_wait(barrier, count)


def remote(src, dst, send, recv, device):
    return pltpu.make_async_remote_copy(
        src_ref=src, dst_ref=dst, send_sem=send, recv_sem=recv,
        device_id=device, device_id_type=MESH,
    )


def fused_kernel(
    blks, rows, cols,
    off_ref, q_ref, k_ref, v_ref, cq_ref, ck_ref, cv_ref, g_ref, m_ref,
    o_out, gq_out, gk_out, gv_out, gcq_out, gck_out, gcv_out,
    side, ext, mask_ext, bias, y_stage, t_stage, low_stage, high_stage, core, recv,
    local_sem, mask_send, mask_recv, in_send, in_recv,
    low_send, low_recv, high_send, high_recv,
    out_send, out_recv, glow_send, glow_recv, ghigh_send, ghigh_recv,
):
    tower, blk, seq, peers = places()
    half, wide = rows, 2 * HEAD
    keys, groups = 3 * rows, cols // (2 * HEAD)
    scale = HEAD ** (-0.5)
    has_low, has_high = blk > 0, blk < blks - 1
    here = pl.ds(pl.multiple_of(seq * half, half), half)
    ext_here = pl.ds(pl.multiple_of((1 + seq) * half, half), half)
    mine = pl.ds(pl.multiple_of(seq * cols, cols), cols)
    inner_low, inner_high = pl.ds(half, half), pl.ds(2 * half, half)
    outer_low, outer_high = pl.ds(0, half), pl.ds(3 * half, half)
    direct = [o_out, gq_out, gcq_out]
    grads = [gk_out, gv_out, gck_out, gcv_out]

    def strip(g, base=0):
        return pl.ds(pl.multiple_of(base + g * wide, wide), wide)

    def incoming(g):
        at = strip(g)
        keep, give = strip(g, seq * cols), strip(g, (1 - seq) * cols)
        moves = [
            (k_ref.at[:, give], ext.at[0, ext_here, at], "y"),
            (v_ref.at[:, give], ext.at[1, ext_here, at], "y"),
            (ck_ref.at[:, give], ext.at[2, ext_here, at], "diag"),
            (cv_ref.at[:, give], ext.at[3, ext_here, at], "diag"),
            (ck_ref.at[:, keep], ext.at[2, ext_here, at], "tower"),
            (cv_ref.at[:, keep], ext.at[3, ext_here, at], "tower"),
            (q_ref.at[:, give], side.at[0, here, at], "y"),
            (g_ref.at[:, give], side.at[2, here, at], "y"),
            (cq_ref.at[:, give], side.at[1, here, at], "y"),
        ]
        return [
            remote(src, dst, in_send.at[g, i], in_recv.at[g, i], peers[to])
            for i, (src, dst, to) in enumerate(moves)
        ]

    def up(g, i):
        at = strip(g)
        return remote(
            ext.at[i, inner_high, at], ext.at[i, outer_low, at],
            high_send.at[g, i], high_recv.at[g, i], peers["high"],
        )

    def down(g, i):
        at = strip(g)
        return remote(
            ext.at[i, inner_low, at], ext.at[i, outer_high, at],
            low_send.at[g, i], low_recv.at[g, i], peers["low"],
        )

    mask_y = remote(m_ref, mask_ext.at[1 + seq], mask_send.at[0], mask_recv.at[0], peers["y"])
    mask_up = remote(mask_ext.at[2], mask_ext.at[0], mask_send.at[1], mask_recv.at[1], peers["high"])
    mask_down = remote(mask_ext.at[1], mask_ext.at[3], mask_send.at[2], mask_recv.at[2], peers["low"])

    def pass_on(g, own):
        moved = incoming(g)
        to_high = (seq == 1) if own else (seq == 0)
        to_low = (seq == 0) if own else (seq == 1)
        for i in range(4):
            if not own:
                moved[i].wait_recv()
            elif i >= 2:
                moved[i + 2].wait_recv()

            @pl.when(to_high & has_high)
            def _():
                up(g, i).start()

            @pl.when(to_low & has_low)
            def _():
                down(g, i).start()

    locals_ = [
        pltpu.make_async_copy(k_ref.at[:, mine], ext.at[0, ext_here, :], local_sem.at[0]),
        pltpu.make_async_copy(v_ref.at[:, mine], ext.at[1, ext_here, :], local_sem.at[1]),
        pltpu.make_async_copy(m_ref, mask_ext.at[1 + seq], local_sem.at[2]),
        pltpu.make_async_copy(q_ref.at[:, mine], side.at[0, here, :], local_sem.at[3]),
        pltpu.make_async_copy(cq_ref.at[:, mine], side.at[1, here, :], local_sem.at[4]),
        pltpu.make_async_copy(g_ref.at[:, mine], side.at[2, here, :], local_sem.at[5]),
    ]
    for copy in locals_:
        copy.start()

    @pl.when(blk == 0)
    def _():
        ext[:, :half, :] = jnp.zeros((4, half, cols), BF16)
        mask_ext[0] = jnp.zeros(mask_ext.shape[1:], jnp.int32)
        recv[0] = jnp.zeros(recv.shape[1:], BF16)

    @pl.when(blk == blks - 1)
    def _():
        ext[:, 3 * half :, :] = jnp.zeros((4, half, cols), BF16)
        mask_ext[3] = jnp.zeros(mask_ext.shape[1:], jnp.int32)
        recv[1] = jnp.zeros(recv.shape[1:], BF16)

    greet(blk, blks, peers)
    mask_y.start()
    for g in range(groups):
        for copy in incoming(g)[:6]:
            copy.start()
    for g in range(groups):
        for copy in incoming(g)[6:]:
            copy.start()
    for copy in locals_:
        copy.wait()
    pass_on(0, True)
    mask_y.wait_recv()

    @pl.when(has_high)
    def _():
        mask_up.start()

    @pl.when(has_low)
    def _():
        mask_down.start()

    for g in range(1, groups):
        pass_on(g, True)
    for g in range(groups):
        pass_on(g, False)

    @pl.when(has_high)
    def _():
        mask_down.wait_recv()

    @pl.when(has_low)
    def _():
        mask_up.wait_recv()

    off = off_ref[tower, blk]
    below = off < 0
    cross_at = jnp.where(below, 0, half)
    band_low = off + half

    def column(part, chain):
        row = jnp.where(
            chain == 0, mask_ext[part, 0:1, :].astype(F32), mask_ext[part, 1:2, :].astype(F32)
        )
        return jnp.transpose(jnp.broadcast_to(row, (half, half)))

    own_valid = [column(part, tower) for part in range(4)]
    other_valid = [column(part, 1 - tower) for part in range(4)]
    row_at = lax.broadcasted_iota(jnp.int32, (half, half), 0)
    col_at = lax.broadcasted_iota(jnp.int32, (half, half), 1)
    for part in range(3):
        where = slice(part * half, (part + 1) * half)
        distance = col_at + half - (row_at + part * half)
        for tile in range(2):
            near = (jnp.abs(distance) <= half) & (own_valid[tile + part] > 0)
            add = jnp.where(near, 0.0, -1e30)
            bias[tile, where, :half] = add
            bias[tile, where, half:] = add
        at = row_at + part * half + cross_at
        valid = jnp.where(below, other_valid[part], other_valid[part + 1])
        inside = (at >= band_low) & (at < band_low + 2 * half) & (valid > 0)
        add = jnp.where(inside, 0.0, -1e30)
        bias[2, where, :half] = add
        bias[2, where, half:] = add

    lanes = lax.broadcasted_iota(jnp.int32, (half, wide), 1)
    zero = jnp.zeros((half, wide), BF16)
    zero_half = jnp.zeros((half, wide), F32)

    def split(tile):
        return jnp.concatenate(
            (jnp.where(lanes < HEAD, tile, zero), jnp.where(lanes < HEAD, zero, tile)), 0
        )

    def dot_t(a, b):
        return lax.dot_general(a, b, (((1,), (1,)), ((), ())), preferred_element_type=F32)

    def dot(a, b):
        return jnp.dot(a, b, preferred_element_type=F32)

    def own_heads(both):
        return jnp.concatenate((both[:HEAD, :half], both[HEAD:, half:]), 0)

    def turned(x):
        return jnp.transpose(x.astype(F32)).astype(BF16)

    def one(query, cot, key, value, key_t, value_t, add):
        scores = dot_t(key, query) + bias[add]
        unnormed = jnp.exp(scores - jnp.max(scores, axis=0, keepdims=True))
        weights = unnormed * (1.0 / jnp.sum(unnormed, axis=0, keepdims=True))
        prob = weights.astype(BF16)
        grad_probs = dot_t(value, cot)
        row_dot = jnp.sum(weights * grad_probs, axis=0, keepdims=True)
        grad_scores = (weights * (grad_probs - row_dot)).astype(BF16)
        result = own_heads(dot(value_t, prob))
        grad_query = own_heads(dot(key_t, grad_scores)) * scale
        return result, grad_query, dot(grad_scores, query), dot(prob, cot)

    def compute(g):
        at = strip(g)
        key, value = ext[0, :, at], ext[1, :, at]
        ckey = jnp.where(below, ext[2, :keys, at], ext[2, half:, at])
        cvalue = jnp.where(below, ext[3, :keys, at], ext[3, half:, at])
        key_t, value_t, ckey_t, cvalue_t = turned(key), turned(value), turned(ckey), turned(cvalue)
        grad_parts, head_parts = [], []
        for tile in range(2):
            span = slice(tile * half, tile * half + keys)
            part = slice(tile * half, (tile + 1) * half)
            cot = split(side[2, part, at])
            query = split(side[0, part, at] * BF16(scale))
            cross = split(side[1, part, at] * BF16(scale))
            so, sq, sk, sv = one(
                query, cot, key[span], value[span], key_t[:, span], value_t[:, span], tile
            )
            co, cq, ck, cv = one(cross, cot, ckey, cvalue, ckey_t, cvalue_t, 2)
            head_parts.append((so + co, sq, cq))
            grad_parts.append((sk, sv, ck, cv))
        for i in range(2):
            first, second = grad_parts[0][i], grad_parts[1][i]
            low_stage[i, :, at] = first[:half].astype(BF16)
            core[i, 0, :, at] = first[half : 2 * half] + second[:half]
            core[i, 1, :, at] = first[2 * half :] + second[half : 2 * half]
            high_stage[i, :, at] = second[2 * half :].astype(BF16)
        for i in range(2, 4):
            total = grad_parts[0][i] + grad_parts[1][i]
            a, b, c = total[:half], total[half : 2 * half], total[2 * half :]
            low_stage[i, :, at] = jnp.where(below, a, zero_half).astype(BF16)
            core[i, 0, :, at] = jnp.where(below, b, a)
            core[i, 1, :, at] = jnp.where(below, c, b)
            high_stage[i, :, at] = jnp.where(below, zero_half, c).astype(BF16)
        for i in range(3):
            lower = turned(head_parts[0][i])
            upper = turned(head_parts[1][i])
            direct[i][:, strip(g, seq * cols)] = jnp.where(seq == 0, lower, upper)
            y_stage[i, :, at] = jnp.where(seq == 0, upper, lower)

    def grad_down(g, i):
        at = strip(g)
        return remote(
            low_stage.at[i, :, at], recv.at[1, i, :, at],
            glow_send.at[g, i], glow_recv.at[g, i], peers["low"],
        )

    def grad_up(g, i):
        at = strip(g)
        return remote(
            high_stage.at[i, :, at], recv.at[0, i, :, at],
            ghigh_send.at[g, i], ghigh_recv.at[g, i], peers["high"],
        )

    def outgoing(g):
        at, to_at = strip(g), strip(g, seq * cols)
        moves = [(y_stage.at[i, :, at], direct[i].at[:, to_at], "y") for i in range(3)]
        moves += [
            (y_stage.at[3 + i, :, at], grads[i].at[:, to_at], "y" if i < 2 else "diag")
            for i in range(4)
        ]
        moves += [(t_stage.at[i, :, at], grads[2 + i].at[:, to_at], "tower") for i in range(2)]
        return [
            remote(src, dst, out_send.at[g, i], out_recv.at[g, i], peers[to])
            for i, (src, dst, to) in enumerate(moves)
        ]

    def start_down(g):
        @pl.when(has_low)
        def _():
            for i in range(4):
                grad_down(g, i).start()

    def start_up(g):
        @pl.when(has_high)
        def _():
            for i in range(4):
                grad_up(g, i).start()

    def give(g):
        @pl.when(seq == 0)
        def _():
            start_down(g)
            start_up(g)

        @pl.when(seq == 1)
        def _():
            start_up(g)
            start_down(g)

        for copy in outgoing(g)[:3]:
            copy.start()

    def finish(g):
        at = strip(g)
        moves = outgoing(g)

        def take(low_side, high_side, i):
            @pl.when(low_side & has_low)
            def _():
                grad_up(g, i).wait_recv()

            @pl.when(high_side & has_high)
            def _():
                grad_down(g, i).wait_recv()

        for i in range(4):
            take(seq == 1, seq == 0, i)
            y_stage[3 + i, :, at] = (
                core[i, 1 - seq, :, at] + recv[1 - seq, i, :, at].astype(F32)
            ).astype(BF16)
            moves[3 + i].start()
        for i in (2, 3, 0, 1):
            take(seq == 0, seq == 1, i)
            total = (core[i, seq, :, at] + recv[seq, i, :, at].astype(F32)).astype(BF16)
            if i < 2:
                grads[i][:, strip(g, seq * cols)] = total
            else:
                t_stage[i - 2, :, at] = total
                moves[5 + i].start()

    def step(g, carry):
        for copy in incoming(g)[6:]:
            copy.wait_recv()

        @pl.when(has_high)
        def _():
            for i in range(4):
                down(g, i).wait_recv()

        @pl.when(has_low)
        def _():
            for i in range(4):
                up(g, i).wait_recv()

        compute(g)
        give(g)

        return carry

    lax.fori_loop(0, groups, step, 0)
    for g in range(groups):
        finish(g)

    def close(g, carry):
        for copy in incoming(g):
            copy.wait_send()
        for copy in outgoing(g):
            copy.wait()

        @pl.when(has_high)
        def _():
            for i in range(4):
                up(g, i).wait_send()
                grad_up(g, i).wait_send()

        @pl.when(has_low)
        def _():
            for i in range(4):
                down(g, i).wait_send()
                grad_down(g, i).wait_send()

        return carry

    lax.fori_loop(0, groups, close, 0)
    mask_y.wait_send()

    @pl.when(has_high)
    def _():
        mask_up.wait_send()

    @pl.when(has_low)
    def _():
        mask_down.wait_send()


def copy_kernel(*refs):
    count = len(refs) // 2
    for src, dst in zip(refs[:count], refs[count:]):
        dst[...] = src[...]


def paired(
    queries, key_rows, value_rows, cross_queries, cross_keys, cross_values, grad_out,
    offsets, key_valid,
):
    blks = lax.axis_size("blk")
    cols = HEADS // lax.axis_size("seq") * HEAD
    values = [
        value[0] for value in (
            queries, key_rows, value_rows, cross_queries, cross_keys, cross_values, grad_out
        )
    ]
    rows = queries.shape[1]
    block, groups = 2 * rows, cols // (2 * HEAD)
    vmem = pl.BlockSpec(memory_space=pltpu.VMEM)
    dma = pltpu.SemaphoreType.DMA
    full = jax.ShapeDtypeStruct((rows, 2 * cols), BF16)
    outs = pl.pallas_call(
        functools.partial(fused_kernel, blks, rows, cols),
        out_shape=(full,) * 7,
        in_specs=[pl.BlockSpec(memory_space=pltpu.SMEM)] + [pl.BlockSpec(memory_space=pl.ANY)] * 8,
        out_specs=(vmem,) * 7,
        scratch_shapes=[
            pltpu.VMEM((3, block, cols), BF16),
            pltpu.VMEM((4, 2 * block, cols), BF16),
            pltpu.VMEM((4,) + key_valid.shape, jnp.int32),
            pltpu.VMEM((3, 3 * rows, block), F32),
            pltpu.VMEM((7, rows, cols), BF16),
            pltpu.VMEM((2, rows, cols), BF16),
            pltpu.VMEM((4, rows, cols), BF16),
            pltpu.VMEM((4, rows, cols), BF16),
            pltpu.VMEM((4, 2, rows, cols), F32),
            pltpu.VMEM((2, 4, rows, cols), BF16),
            dma((6,)), dma((3,)), dma((3,)),
            dma((groups, 9)), dma((groups, 9)),
            dma((groups, 4)), dma((groups, 4)), dma((groups, 4)), dma((groups, 4)),
            dma((groups, 9)), dma((groups, 9)),
            dma((groups, 4)), dma((groups, 4)), dma((groups, 4)), dma((groups, 4)),
        ],
        compiler_params=pltpu.CompilerParams(collective_id=0, has_side_effects=True),
        name="attend_pairs",
    )(offsets, *values, key_valid)
    outs = pl.pallas_call(
        copy_kernel,
        out_shape=(full,) * 7,
        in_specs=[vmem] * 7,
        out_specs=(vmem,) * 7,
        name="hand_over",
    )(*outs)
    return tuple(piece[None] for piece in outs)


def extended(block, sides, width):
    for axis, dim in sides:
        count = lax.axis_size(axis)
        forward = [(i, i + 1) for i in range(count - 1)]
        backward = [(target, source) for source, target in forward]
        low = lax.ppermute(
            lax.slice_in_dim(block, block.shape[dim] - width, None, axis=dim), axis, forward
        )
        high = lax.ppermute(lax.slice_in_dim(block, 0, width, axis=dim), axis, backward)
        block = jnp.concatenate([low, block, high], axis=dim)
    return block


def swapped(value, axis, bit):
    mask = 2**bit
    pairs = [(source, source ^ mask) for source in range(lax.axis_size(axis))]
    return lax.ppermute(value, axis, pairs)


def passed_along(block, axis, distance):
    devices = range(lax.axis_size(axis))
    route = [(i - distance, i) for i in devices if i - distance in devices]
    return lax.ppermute(block, axis, route)


def attend(query_tile, grad_tile, key_block, value_block, allowed, heads_here):
    score_scale = HEAD ** (-0.5)
    rows_count = query_tile.shape[0]
    keys_count = key_block.shape[0]
    q_heads = query_tile.reshape(rows_count, heads_here, HEAD)
    g_heads = grad_tile.reshape(rows_count, heads_here, HEAD)
    k_heads = key_block.reshape(keys_count, heads_here, HEAD)
    v_heads = value_block.reshape(keys_count, heads_here, HEAD)
    scores = (
        jnp.einsum("qhe,khe->hqk", q_heads, k_heads, preferred_element_type=jnp.float32)
        * score_scale
    )
    scores = jnp.where(allowed[None], scores, -1e30)
    row_max = jnp.max(scores, axis=2)
    unnormed = jnp.exp(scores - row_max[:, :, None])
    row_sum = jnp.sum(unnormed, axis=2)
    weights = unnormed / row_sum[:, :, None]
    prob_bf = weights.astype(jnp.bfloat16)
    result = jnp.einsum(
        "hqk,khe->qhe", prob_bf, v_heads, preferred_element_type=jnp.float32
    ).reshape(rows_count, -1)
    grad_probs = jnp.einsum("qhe,khe->hqk", g_heads, v_heads, preferred_element_type=jnp.float32)
    row_dot = jnp.sum(weights * grad_probs, axis=2)
    grad_scores = (weights * (grad_probs - row_dot[:, :, None]) * score_scale).astype(jnp.bfloat16)
    grad_query = jnp.einsum(
        "hqk,khe->qhe", grad_scores, k_heads, preferred_element_type=jnp.float32
    ).reshape(rows_count, -1)
    grad_key = jnp.einsum(
        "hqk,qhe->khe", grad_scores, q_heads, preferred_element_type=jnp.float32
    ).reshape(keys_count, -1)
    grad_value = jnp.einsum(
        "hqk,qhe->khe", prob_bf, g_heads, preferred_element_type=jnp.float32
    ).reshape(keys_count, -1)
    return (result, grad_query, grad_key, grad_value, jnp.stack((row_max, row_sum, row_dot)))


def shards(
    queries,
    key_rows,
    value_rows,
    cross_queries,
    cross_keys,
    cross_values,
    grad_out,
    offsets,
    key_valid,
):
    seq_count = lax.axis_size("seq")
    heads_here = HEADS // seq_count
    local_rows = (
        queries[0],
        key_rows[0],
        value_rows[0],
        cross_queries[0],
        cross_keys[0],
        cross_values[0],
        grad_out[0],
    )
    query_here, key_here, value_here, cross_query, cross_key, cross_value, cotangent = (
        lax.all_to_all(local_rows[0], "seq", split_axis=1, concat_axis=0, tiled=True),
        lax.all_to_all(local_rows[1], "seq", split_axis=1, concat_axis=0, tiled=True),
        lax.all_to_all(local_rows[2], "seq", split_axis=1, concat_axis=0, tiled=True),
        lax.all_to_all(local_rows[3], "seq", split_axis=1, concat_axis=0, tiled=True),
        lax.all_to_all(local_rows[4], "seq", split_axis=1, concat_axis=0, tiled=True),
        lax.all_to_all(local_rows[5], "seq", split_axis=1, concat_axis=0, tiled=True),
        lax.all_to_all(local_rows[6], "seq", split_axis=1, concat_axis=0, tiled=True),
    )
    block_len = query_here.shape[0]
    columns = query_here.shape[1]
    half_width = min(WINDOW // 2, block_len // 2)
    tile_rows = min(TILE, block_len)
    tile_count = block_len // tile_rows
    window_span = tile_rows + 2 * half_width
    tower_id = lax.axis_index("tower")
    block_id = lax.axis_index("blk")
    block_mask = lax.all_gather(key_valid, "seq", axis=1, tiled=True)
    mask_ext = extended(block_mask, (("blk", 1),), half_width)
    self_valid = lax.dynamic_index_in_dim(mask_ext, tower_id, 0, keepdims=False)
    other_valid = lax.dynamic_index_in_dim(mask_ext, 1 - tower_id, 0, keepdims=False)
    pair_ext = extended(jnp.stack((key_here, value_here)), (("blk", 1),), half_width)
    partner = swapped(jnp.stack((cross_key, cross_value)), "tower", 0)
    partner_ext = extended(partner, (("blk", 1),), half_width)
    align_shift = offsets[tower_id, block_id]
    band_start = half_width + align_shift
    band = lax.dynamic_slice_in_dim(partner_ext, band_start, block_len, 1)
    band_valid = lax.dynamic_slice_in_dim(other_valid, band_start, block_len) > 0
    rows_local = jnp.arange(tile_rows)
    keys_local = jnp.arange(window_span)
    near = jnp.abs(rows_local[:, None] + half_width - keys_local[None, :]) <= half_width

    def self_step(carry, tile_index):
        grad_key_acc, grad_value_acc = carry
        tile_start = tile_index * tile_rows
        query_tile = lax.dynamic_slice_in_dim(query_here, tile_start, tile_rows, 0)
        grad_tile = lax.dynamic_slice_in_dim(cotangent, tile_start, tile_rows, 0)
        key_window = lax.dynamic_slice_in_dim(pair_ext[0], tile_start, window_span, 0)
        value_window = lax.dynamic_slice_in_dim(pair_ext[1], tile_start, window_span, 0)
        allowed = (
            near & (lax.dynamic_slice_in_dim(self_valid, tile_start, window_span) > 0)[None, :]
        )
        result, grad_query, grad_key, grad_value, stats = attend(
            query_tile, grad_tile, key_window, value_window, allowed, heads_here
        )
        grad_key_acc = lax.dynamic_update_slice_in_dim(
            grad_key_acc,
            lax.dynamic_slice_in_dim(grad_key_acc, tile_start, window_span, 0) + grad_key,
            tile_start,
            0,
        )
        grad_value_acc = lax.dynamic_update_slice_in_dim(
            grad_value_acc,
            lax.dynamic_slice_in_dim(grad_value_acc, tile_start, window_span, 0) + grad_value,
            tile_start,
            0,
        )
        return ((grad_key_acc, grad_value_acc), (result, grad_query, stats))

    def cross_step(carry, tile_index):
        grad_key_acc, grad_value_acc = carry
        tile_start = tile_index * tile_rows
        query_tile = lax.dynamic_slice_in_dim(cross_query, tile_start, tile_rows, 0)
        grad_tile = lax.dynamic_slice_in_dim(cotangent, tile_start, tile_rows, 0)
        result, grad_query, grad_key, grad_value, stats = attend(
            query_tile, grad_tile, band[0], band[1], band_valid[None, :], heads_here
        )
        return ((grad_key_acc + grad_key, grad_value_acc + grad_value), (result, grad_query))

    zeros_ext = jnp.zeros((block_len + 2 * half_width, columns), jnp.float32)
    zeros_band = jnp.zeros((block_len, columns), jnp.float32)
    tile_ids = jnp.arange(tile_count)
    (self_gk, self_gv), (self_out, self_gq, self_stats) = lax.scan(
        self_step, (zeros_ext, zeros_ext), tile_ids
    )
    (cross_gk, cross_gv), (cross_out, cross_gq) = lax.scan(
        cross_step, (zeros_band, zeros_band), tile_ids
    )
    self_out = self_out.reshape(block_len, columns)
    cross_out = cross_out.reshape(block_len, columns)
    self_stats = jnp.transpose(self_stats, (1, 2, 0, 3)).reshape(3, heads_here, block_len)
    attended = (self_out + cross_out).astype(jnp.bfloat16)
    cross_ext = jnp.zeros((2, block_len + 2 * half_width, columns), jnp.float32)
    cross_ext = lax.dynamic_update_slice_in_dim(
        cross_ext, jnp.stack((cross_gk, cross_gv)), band_start, 1
    )
    self_ext = jnp.stack((self_gk, self_gv))
    self_core = self_ext[:, half_width : half_width + block_len]
    cross_core = cross_ext[:, half_width : half_width + block_len]
    upper_cut = block_len - half_width
    lower_send = jnp.concatenate((self_ext[:, :half_width], cross_ext[:, :half_width]), 0)
    upper_send = jnp.concatenate(
        (self_ext[:, block_len + half_width :], cross_ext[:, block_len + half_width :]), 0
    )
    from_above = passed_along(lower_send.astype(jnp.bfloat16), "blk", -1).astype(lower_send.dtype)
    from_below = passed_along(upper_send.astype(jnp.bfloat16), "blk", 1).astype(upper_send.dtype)
    self_core = (
        self_core.at[:, upper_cut:].add(from_above[:2]).at[:, :half_width].add(from_below[:2])
    )
    cross_core = (
        cross_core.at[:, upper_cut:].add(from_above[2:]).at[:, :half_width].add(from_below[2:])
    )
    returned = swapped(cross_core.astype(jnp.bfloat16), "tower", 0)
    head_outs = (
        attended,
        self_gq.reshape(block_len, columns).astype(jnp.bfloat16),
        self_core[0].astype(jnp.bfloat16),
        self_core[1].astype(jnp.bfloat16),
        cross_gq.reshape(block_len, columns).astype(jnp.bfloat16),
        returned[0],
        returned[1],
    )
    token_outs = (
        lax.all_to_all(head_outs[0], "seq", split_axis=0, concat_axis=1, tiled=True),
        lax.all_to_all(head_outs[1], "seq", split_axis=0, concat_axis=1, tiled=True),
        lax.all_to_all(head_outs[2], "seq", split_axis=0, concat_axis=1, tiled=True),
        lax.all_to_all(head_outs[3], "seq", split_axis=0, concat_axis=1, tiled=True),
        lax.all_to_all(head_outs[4], "seq", split_axis=0, concat_axis=1, tiled=True),
        lax.all_to_all(head_outs[5], "seq", split_axis=0, concat_axis=1, tiled=True),
        lax.all_to_all(head_outs[6], "seq", split_axis=0, concat_axis=1, tiled=True),
    )
    return tuple((piece[None] for piece in token_outs))


def solution(mesh):
    in_specs = (
        P("tower", ("blk", "seq"), None),
        P("tower", ("blk", "seq"), None),
        P("tower", ("blk", "seq"), None),
        P("tower", ("blk", "seq"), None),
        P("tower", ("blk", "seq"), None),
        P("tower", ("blk", "seq"), None),
        P("tower", ("blk", "seq"), None),
        P(),
        P(None, ("blk", "seq")),
    )
    out_specs = (
        P("tower", ("blk", "seq"), None),
        P("tower", ("blk", "seq"), None),
        P("tower", ("blk", "seq"), None),
        P("tower", ("blk", "seq"), None),
        P("tower", ("blk", "seq"), None),
        P("tower", ("blk", "seq"), None),
        P("tower", ("blk", "seq"), None),
    )
    body = paired if mesh.shape["seq"] == 2 else shards
    return jax.shard_map(body, mesh=mesh, in_specs=in_specs, out_specs=out_specs, check_vma=False)
```

profile of v0, /device:TPU:9, one launch (start us, length us, event | category | flops | bytes accessed | tf_op | source)
XLA Modules:
  0.0 61.1 jit_solution(14575381427242455293)
XLA Ops:
  0.6 57.8 %attend_pairs.1 = (bf16[128,1024]{1,0:T(8,128)(2,1)}, bf16[128,1024]{1,0:T(8,128)(2,1)}, bf16[128,1024]{1,0:T(8,128)(2,1)}, bf16[128,1024]{1,0:T(8,128)(2,1)}, b...) custom-call(s32[2,8]{1,0:T(2,128)} %off_ref.1, bf16[128,1024]{1,0:T(8,128)(2,1)} %bitcast.14, ...), custom_call_target="tpu_custom_call" | custom-call | tf_op jit(solution)/shard_map/attend_pairs/pallas_call | solution.py:450
  58.4 2.7 %hand_over.1 = (bf16[128,1024]{1,0:T(8,128)(2,1)}, bf16[128,1024]{1,0:T(8,128)(2,1)}, bf16[128,1024]{1,0:T(8,128)(2,1)}, bf16[128,1024]{1,0:T(8,128)(2,1)}, bf16...) custom-call(bf16[128,1024]{1,0:T(8,128)(2,1)} %get-tuple-element.21.refs_0_, ...), custom_call_target="tpu_custom_call" | custom-call | tf_op jit(solution)/shard_map/hand_over/pallas_call | solution.py:475
where the time goes:
time: 61.2 us; the launch traced here: 61.1 us
  Pallas kernels  60.4 us (99%)
  between operations  0.64 us (1%)
    pallas_call x1, Pallas kernels, paired(): pl.pallas_call(functools.partial(fused_kernel, blks, rows, cols), out_sha...  57.8 us
    pallas_call x1, Pallas kernels, paired(): pl.pallas_call(copy_kernel, out_shape=(full,) * 7, in_specs=[vmem] * 7, o...  2.67 us

commit v1 on v0

--- a/solution.py
+++ b/solution.py
@@ -11,6 +11,7 @@
 HEAD = 64
 WINDOW = 2048
 TILE = 512
+LAG = 2
 MESH = pl.DeviceIdType.MESH
 F32, BF16 = jnp.float32, jnp.bfloat16
 
@@ -55,10 +56,12 @@
     blks, rows, cols,
     off_ref, q_ref, k_ref, v_ref, cq_ref, ck_ref, cv_ref, g_ref, m_ref,
     o_out, gq_out, gk_out, gv_out, gcq_out, gck_out, gcv_out,
-    side, ext, mask_ext, bias, y_stage, t_stage, low_stage, high_stage, core, recv,
+    side, ext, cext, mate, pick, far, mask_ext, bias,
+    y_stage, t_stage, low_stage, high_stage, core, recv, part, mate_part, gpick, gfar,
     local_sem, mask_send, mask_recv, in_send, in_recv,
-    low_send, low_recv, high_send, high_recv,
+    low_send, low_recv, high_send, high_recv, mate_send, mate_recv, far_send, far_recv,
     out_send, out_recv, glow_send, glow_recv, ghigh_send, ghigh_recv,
+    part_send, part_recv, gfar_send, gfar_recv,
 ):
     tower, blk, seq, peers = places()
     half, wide = rows, 2 * HEAD
@@ -73,6 +76,11 @@
     direct = [o_out, gq_out, gcq_out]
     grads = [gk_out, gv_out, gck_out, gcv_out]
 
+    off = off_ref[tower, blk]
+    off_below = off_ref[tower, jnp.maximum(blk - 1, 0)]
+    off_above = off_ref[tower, jnp.minimum(blk + 1, blks - 1)]
+    below = off < 0
+
     def strip(g, base=0):
         return pl.ds(pl.multiple_of(base + g * wide, wide), wide)
 
@@ -82,10 +90,10 @@
         moves = [
             (k_ref.at[:, give], ext.at[0, ext_here, at], "y"),
             (v_ref.at[:, give], ext.at[1, ext_here, at], "y"),
-            (ck_ref.at[:, give], ext.at[2, ext_here, at], "diag"),
-            (cv_ref.at[:, give], ext.at[3, ext_here, at], "diag"),
-            (ck_ref.at[:, keep], ext.at[2, ext_here, at], "tower"),
-            (cv_ref.at[:, keep], ext.at[3, ext_here, at], "tower"),
+            (ck_ref.at[:, give], cext.at[0, here, at], "diag"),
+            (cv_ref.at[:, give], cext.at[1, here, at], "diag"),
+            (ck_ref.at[:, keep], cext.at[0, here, at], "tower"),
+            (cv_ref.at[:, keep], cext.at[1, here, at], "tower"),
             (q_ref.at[:, give], side.at[0, here, at], "y"),
             (g_ref.at[:, give], side.at[2, here, at], "y"),
             (cq_ref.at[:, give], side.at[1, here, at], "y"),
@@ -97,39 +105,56 @@
 
     def up(g, i):
         at = strip(g)
+        if i < 2:
+            src, dst = ext.at[i, inner_high, at], ext.at[i, outer_low, at]
+        else:
+            src, dst = pick.at[1, :, at], far.at[0, tower, :, at]
+        return remote(src, dst, high_send.at[g, i], high_recv.at[g, i], peers["high"])
+
+    def down(g, i):
+        at = strip(g)
+        if i < 2:
+            src, dst = ext.at[i, inner_low, at], ext.at[i, outer_high, at]
+        else:
+            src, dst = pick.at[0, :, at], far.at[1, tower, :, at]
+        return remote(src, dst, low_send.at[g, i], low_recv.at[g, i], peers["low"])
+
+    def mated(g):
+        at = strip(g)
+        other = pl.ds(pl.multiple_of((1 - seq) * half, half), half)
         return remote(
-            ext.at[i, inner_high, at], ext.at[i, outer_low, at],
-            high_send.at[g, i], high_recv.at[g, i], peers["high"],
-        )
-
-    def down(g, i):
+            cext.at[1 - tower, other, at], mate.at[other, at],
+            mate_send.at[g], mate_recv.at[g], peers["tower"],
+        )
+
+    def shared(g, i):
         at = strip(g)
         return remote(
-            ext.at[i, inner_low, at], ext.at[i, outer_high, at],
-            low_send.at[g, i], low_recv.at[g, i], peers["low"],
+            far.at[i, tower, :, at], far.at[i, tower, :, at],
+            far_send.at[g, i], far_recv.at[g, i], peers["tower"],
         )
 
     mask_y = remote(m_ref, mask_ext.at[1 + seq], mask_send.at[0], mask_recv.at[0], peers["y"])
     mask_up = remote(mask_ext.at[2], mask_ext.at[0], mask_send.at[1], mask_recv.at[1], peers["high"])
     mask_down = remote(mask_ext.at[1], mask_ext.at[3], mask_send.at[2], mask_recv.at[2], peers["low"])
 
-    def pass_on(g, own):
-        moved = incoming(g)
-        to_high = (seq == 1) if own else (seq == 0)
-        to_low = (seq == 0) if own else (seq == 1)
-        for i in range(4):
-            if not own:
-                moved[i].wait_recv()
-            elif i >= 2:
-                moved[i + 2].wait_recv()
-
-            @pl.when(to_high & has_high)
-            def _():
-                up(g, i).start()
-
-            @pl.when(to_low & has_low)
-            def _():
-                down(g, i).start()
+    def pass_on(g, i, own):
+        @pl.when(((seq == 1) if own else (seq == 0)) & has_high)
+        def _():
+            up(g, i).start()
+
+        @pl.when(((seq == 0) if own else (seq == 1)) & has_low)
+        def _():
+            down(g, i).start()
+
+    def choose(g, own):
+        at = strip(g)
+        tile = seq if own else 1 - seq
+        where = here if own else pl.ds(pl.multiple_of((1 - seq) * half, half), half)
+        high = tile == 1
+        chain = jnp.where(high, jnp.where(off_above > 0, 1, 0), jnp.where(off_below < 0, 1, 0))
+        pick[tile, :, at] = jnp.where(chain == 1, mate[where, at], cext[tower, where, at])
+        pass_on(g, 2, own)
 
     locals_ = [
         pltpu.make_async_copy(k_ref.at[:, mine], ext.at[0, ext_here, :], local_sem.at[0]),
@@ -141,30 +166,44 @@
     ]
     for copy in locals_:
         copy.start()
+    for chain, ref in enumerate((ck_ref, cv_ref)):
+        @pl.when(tower == chain)
+        def _():
+            pltpu.make_async_copy(ref.at[:, mine], mate.at[here, :], local_sem.at[6]).start()
 
     @pl.when(blk == 0)
     def _():
-        ext[:, :half, :] = jnp.zeros((4, half, cols), BF16)
+        ext[:, :half, :] = jnp.zeros((2, half, cols), BF16)
+        far[0] = jnp.zeros(far.shape[1:], BF16)
         mask_ext[0] = jnp.zeros(mask_ext.shape[1:], jnp.int32)
         recv[0] = jnp.zeros(recv.shape[1:], BF16)
+        gfar[0] = jnp.zeros(gfar.shape[1:], BF16)
 
     @pl.when(blk == blks - 1)
     def _():
-        ext[:, 3 * half :, :] = jnp.zeros((4, half, cols), BF16)
+        ext[:, 3 * half :, :] = jnp.zeros((2, half, cols), BF16)
+        far[1] = jnp.zeros(far.shape[1:], BF16)
         mask_ext[3] = jnp.zeros(mask_ext.shape[1:], jnp.int32)
         recv[1] = jnp.zeros(recv.shape[1:], BF16)
+        gfar[1] = jnp.zeros(gfar.shape[1:], BF16)
+
+    for copy in locals_:
+        copy.wait()
+    for chain, ref in enumerate((ck_ref, cv_ref)):
+        @pl.when(tower == chain)
+        def _():
+            pltpu.make_async_copy(ref.at[:, mine], mate.at[here, :], local_sem.at[6]).wait()
 
     greet(blk, blks, peers)
     mask_y.start()
     for g in range(groups):
         for copy in incoming(g)[:6]:
             copy.start()
+        for i in range(2):
+            pass_on(g, i, True)
     for g in range(groups):
         for copy in incoming(g)[6:]:
             copy.start()
-    for copy in locals_:
-        copy.wait()
-    pass_on(0, True)
     mask_y.wait_recv()
 
     @pl.when(has_high)
@@ -175,10 +214,23 @@
     def _():
         mask_down.start()
 
-    for g in range(1, groups):
-        pass_on(g, True)
     for g in range(groups):
-        pass_on(g, False)
+        for copy in incoming(g)[4:6]:
+            copy.wait_recv()
+        choose(g, True)
+    for g in range(groups):
+        moved = incoming(g)
+        for i in range(2):
+            moved[i].wait_recv()
+            pass_on(g, i, False)
+        for i in range(2, 4):
+            moved[i].wait_recv()
+        mated(g).start()
+        if g:
+            mated(g - 1).wait_recv()
+            choose(g - 1, False)
+    mated(groups - 1).wait_recv()
+    choose(groups - 1, False)
 
     @pl.when(has_high)
     def _():
@@ -188,8 +240,6 @@
     def _():
         mask_up.wait_recv()
 
-    off = off_ref[tower, blk]
-    below = off < 0
     cross_at = jnp.where(below, 0, half)
     band_low = off + half
 
@@ -203,16 +253,16 @@
     other_valid = [column(part, 1 - tower) for part in range(4)]
     row_at = lax.broadcasted_iota(jnp.int32, (half, half), 0)
     col_at = lax.broadcasted_iota(jnp.int32, (half, half), 1)
-    for part in range(3):
-        where = slice(part * half, (part + 1) * half)
-        distance = col_at + half - (row_at + part * half)
+    for part_at in range(3):
+        where = slice(part_at * half, (part_at + 1) * half)
+        distance = col_at + half - (row_at + part_at * half)
         for tile in range(2):
-            near = (jnp.abs(distance) <= half) & (own_valid[tile + part] > 0)
+            near = (jnp.abs(distance) <= half) & (own_valid[tile + part_at] > 0)
             add = jnp.where(near, 0.0, -1e30)
             bias[tile, where, :half] = add
             bias[tile, where, half:] = add
-        at = row_at + part * half + cross_at
-        valid = jnp.where(below, other_valid[part], other_valid[part + 1])
+        at = row_at + part_at * half + cross_at
+        valid = jnp.where(below, other_valid[part_at], other_valid[part_at + 1])
         inside = (at >= band_low) & (at < band_low + 2 * half) & (valid > 0)
         add = jnp.where(inside, 0.0, -1e30)
         bias[2, where, :half] = add
@@ -220,7 +270,6 @@
 
     lanes = lax.broadcasted_iota(jnp.int32, (half, wide), 1)
     zero = jnp.zeros((half, wide), BF16)
-    zero_half = jnp.zeros((half, wide), F32)
 
     def split(tile):
         return jnp.concatenate(
@@ -251,38 +300,57 @@
         grad_query = own_heads(dot(key_t, grad_scores)) * scale
         return result, grad_query, dot(grad_scores, query), dot(prob, cot)
 
-    def compute(g):
+    def cots(g):
+        at = strip(g)
+        return [split(side[2, tile * half : (tile + 1) * half, at]) for tile in range(2)]
+
+    def cross_part(g, cot):
+        at = strip(g)
+
+        def band(i):
+            first, second = cext[i, :half, at], cext[i, half:, at]
+            return jnp.concatenate(
+                (
+                    jnp.where(below, far[0, i, :, at], first),
+                    jnp.where(below, first, second),
+                    jnp.where(below, second, far[1, i, :, at]),
+                ),
+                0,
+            )
+
+        ckey, cvalue = band(0), band(1)
+        ckey_t, cvalue_t = turned(ckey), turned(cvalue)
+        results = []
+        for tile in range(2):
+            cross = split(side[1, tile * half : (tile + 1) * half, at] * BF16(scale))
+            results.append(one(cross, cot[tile], ckey, cvalue, ckey_t, cvalue_t, 2))
+        for i in range(2):
+            total = results[0][2 + i] + results[1][2 + i]
+            a, b, c = total[:half], total[half : 2 * half], total[2 * half :]
+            part[i, :, at] = jnp.where(below, a, c).astype(BF16)
+            core[2 + i, 0, :, at] = jnp.where(below, b, a)
+            core[2 + i, 1, :, at] = jnp.where(below, c, b)
+        return [(result[0], result[1]) for result in results]
+
+    def self_part(g, cot, crossed):
         at = strip(g)
         key, value = ext[0, :, at], ext[1, :, at]
-        ckey = jnp.where(below, ext[2, :keys, at], ext[2, half:, at])
-        cvalue = jnp.where(below, ext[3, :keys, at], ext[3, half:, at])
-        key_t, value_t, ckey_t, cvalue_t = turned(key), turned(value), turned(ckey), turned(cvalue)
+        key_t, value_t = turned(key), turned(value)
         grad_parts, head_parts = [], []
         for tile in range(2):
             span = slice(tile * half, tile * half + keys)
-            part = slice(tile * half, (tile + 1) * half)
-            cot = split(side[2, part, at])
-            query = split(side[0, part, at] * BF16(scale))
-            cross = split(side[1, part, at] * BF16(scale))
+            query = split(side[0, tile * half : (tile + 1) * half, at] * BF16(scale))
             so, sq, sk, sv = one(
-                query, cot, key[span], value[span], key_t[:, span], value_t[:, span], tile
+                query, cot[tile], key[span], value[span], key_t[:, span], value_t[:, span], tile
             )
-            co, cq, ck, cv = one(cross, cot, ckey, cvalue, ckey_t, cvalue_t, 2)
-            head_parts.append((so + co, sq, cq))
-            grad_parts.append((sk, sv, ck, cv))
+            head_parts.append((so + crossed[tile][0], sq, crossed[tile][1]))
+            grad_parts.append((sk, sv))
         for i in range(2):
             first, second = grad_parts[0][i], grad_parts[1][i]
             low_stage[i, :, at] = first[:half].astype(BF16)
             core[i, 0, :, at] = first[half : 2 * half] + second[:half]
             core[i, 1, :, at] = first[2 * half :] + second[half : 2 * half]
             high_stage[i, :, at] = second[2 * half :].astype(BF16)
-        for i in range(2, 4):
-            total = grad_parts[0][i] + grad_parts[1][i]
-            a, b, c = total[:half], total[half : 2 * half], total[2 * half :]
-            low_stage[i, :, at] = jnp.where(below, a, zero_half).astype(BF16)
-            core[i, 0, :, at] = jnp.where(below, b, a)
-            core[i, 1, :, at] = jnp.where(below, c, b)
-            high_stage[i, :, at] = jnp.where(below, zero_half, c).astype(BF16)
         for i in range(3):
             lower = turned(head_parts[0][i])
             upper = turned(head_parts[1][i])
@@ -291,16 +359,32 @@
 
     def grad_down(g, i):
         at = strip(g)
+        if i < 2:
+            src, dst = low_stage.at[i, :, at], recv.at[1, i, :, at]
+        else:
+            src, dst = gpick.at[0, :, at], gfar.at[1, tower, :, at]
+        return remote(src, dst, glow_send.at[g, i], glow_recv.at[g, i], peers["low"])
+
+    def grad_up(g, i):
+        at = strip(g)
+        if i < 2:
+            src, dst = high_stage.at[i, :, at], recv.at[0, i, :, at]
+        else:
+            src, dst = gpick.at[1, :, at], gfar.at[0, tower, :, at]
+        return remote(src, dst, ghigh_send.at[g, i], ghigh_recv.at[g, i], peers["high"])
+
+    def swap(g):
+        at = strip(g)
         return remote(
-            low_stage.at[i, :, at], recv.at[1, i, :, at],
-            glow_send.at[g, i], glow_recv.at[g, i], peers["low"],
-        )
-
-    def grad_up(g, i):
+            part.at[1 - tower, :, at], mate_part.at[:, at],
+            part_send.at[g], part_recv.at[g], peers["tower"],
+        )
+
+    def gshared(g, i):
         at = strip(g)
         return remote(
-            high_stage.at[i, :, at], recv.at[0, i, :, at],
-            ghigh_send.at[g, i], ghigh_recv.at[g, i], peers["high"],
+            gfar.at[i, tower, :, at], gfar.at[i, tower, :, at],
+            gfar_send.at[g, i], gfar_recv.at[g, i], peers["tower"],
         )
 
     def outgoing(g):
@@ -319,16 +403,22 @@
     def start_down(g):
         @pl.when(has_low)
         def _():
-            for i in range(4):
+            for i in (2, 0, 1):
                 grad_down(g, i).start()
 
     def start_up(g):
         @pl.when(has_high)
         def _():
-            for i in range(4):
+            for i in (2, 0, 1):
                 grad_up(g, i).start()
 
     def give(g):
+        at = strip(g)
+        swap(g).wait_recv()
+        own, others = part[tower, :, at], mate_part[:, at]
+        gpick[0, :, at] = jnp.where(below, own, others)
+        gpick[1, :, at] = jnp.where(below, others, own)
+
         @pl.when(seq == 0)
         def _():
             start_down(g)
@@ -342,55 +432,111 @@
         for copy in outgoing(g)[:3]:
             copy.start()
 
+    def share(g):
+        @pl.when(has_low)
+        def _():
+            up(g, 2).wait_recv()
+            shared(g, 0).start()
+
+        @pl.when(has_high)
+        def _():
+            down(g, 2).wait_recv()
+            shared(g, 1).start()
+
+    take_low, take_high = off_below > 0, off_above < 0
+
     def finish(g):
         at = strip(g)
         moves = outgoing(g)
 
-        def take(low_side, high_side, i):
+        def on_side(low_side, high_side, low, high):
             @pl.when(low_side & has_low)
             def _():
-                grad_up(g, i).wait_recv()
+                low()
 
             @pl.when(high_side & has_high)
             def _():
-                grad_down(g, i).wait_recv()
-
-        for i in range(4):
-            take(seq == 1, seq == 0, i)
-            y_stage[3 + i, :, at] = (
-                core[i, 1 - seq, :, at] + recv[1 - seq, i, :, at].astype(F32)
-            ).astype(BF16)
+                high()
+
+        def tile_of(tile, low_side, high_side, place):
+            def relay_low():
+                grad_up(g, 2).wait_recv()
+                gshared(g, 0).start()
+
+            def relay_high():
+                grad_down(g, 2).wait_recv()
+                gshared(g, 1).start()
+
+            on_side(low_side, high_side, relay_low, relay_high)
+            for i in range(2):
+                on_side(
+                    low_side, high_side, grad_up(g, i).wait_recv, grad_down(g, i).wait_recv
+                )
+                place(
+                    i, (core[i, tile, :, at] + recv[tile, i, :, at].astype(F32)).astype(BF16)
+                )
+            on_side(low_side, high_side, gshared(g, 0).wait_recv, gshared(g, 1).wait_recv)
+            wanted = jnp.where(low_side, jnp.where(take_low, 1, 0), jnp.where(take_high, 1, 0))
+            for i in range(2):
+                more = jnp.where(wanted == 1, gfar[tile, i, :, at].astype(F32), 0.0)
+                place(2 + i, (core[2 + i, tile, :, at] + more).astype(BF16))
+
+        def give_away(i, total):
+            y_stage[3 + i, :, at] = total
             moves[3 + i].start()
-        for i in (2, 3, 0, 1):
-            take(seq == 0, seq == 1, i)
-            total = (core[i, seq, :, at] + recv[seq, i, :, at].astype(F32)).astype(BF16)
+
+        def keep_here(i, total):
             if i < 2:
                 grads[i][:, strip(g, seq * cols)] = total
             else:
                 t_stage[i - 2, :, at] = total
                 moves[5 + i].start()
 
+        tile_of(1 - seq, seq == 1, seq == 0, give_away)
+        tile_of(seq, seq == 0, seq == 1, keep_here)
+
     def step(g, carry):
         for copy in incoming(g)[6:]:
             copy.wait_recv()
 
+        @pl.when(has_low)
+        def _():
+            shared(g, 0).wait_recv()
+
         @pl.when(has_high)
         def _():
-            for i in range(4):
+            shared(g, 1).wait_recv()
+
+        cot = cots(g)
+        crossed = cross_part(g, cot)
+        swap(g).start()
+
+        @pl.when(g + 1 < groups)
+        def _():
+            share(g + 1)
+
+        @pl.when(has_high)
+        def _():
+            for i in range(2):
                 down(g, i).wait_recv()
 
         @pl.when(has_low)
         def _():
-            for i in range(4):
+            for i in range(2):
                 up(g, i).wait_recv()
 
-        compute(g)
+        self_part(g, cot, crossed)
         give(g)
 
+        @pl.when(g >= LAG)
+        def _():
+            finish(g - LAG)
+
         return carry
 
+    share(0)
     lax.fori_loop(0, groups, step, 0)
-    for g in range(groups):
+    for g in range(max(groups - LAG, 0), groups):
         finish(g)
 
     def close(g, carry):
@@ -398,18 +544,24 @@
             copy.wait_send()
         for copy in outgoing(g):
             copy.wait()
+        mated(g).wait_send()
+        swap(g).wait_send()
 
         @pl.when(has_high)
         def _():
-            for i in range(4):
+            for i in range(3):
                 up(g, i).wait_send()
                 grad_up(g, i).wait_send()
+            shared(g, 1).wait_send()
+            gshared(g, 1).wait_send()
 
         @pl.when(has_low)
         def _():
-            for i in range(4):
+            for i in range(3):
                 down(g, i).wait_send()
                 grad_down(g, i).wait_send()
+            shared(g, 0).wait_send()
+            gshared(g, 0).wait_send()
 
         return carry
 
@@ -454,20 +606,30 @@
         out_specs=(vmem,) * 7,
         scratch_shapes=[
             pltpu.VMEM((3, block, cols), BF16),
-            pltpu.VMEM((4, 2 * block, cols), BF16),
+            pltpu.VMEM((2, 2 * block, cols), BF16),
+            pltpu.VMEM((2, block, cols), BF16),
+            pltpu.VMEM((block, cols), BF16),
+            pltpu.VMEM((2, rows, cols), BF16),
+            pltpu.VMEM((2, 2, rows, cols), BF16),
             pltpu.VMEM((4,) + key_valid.shape, jnp.int32),
             pltpu.VMEM((3, 3 * rows, block), F32),
             pltpu.VMEM((7, rows, cols), BF16),
             pltpu.VMEM((2, rows, cols), BF16),
-            pltpu.VMEM((4, rows, cols), BF16),
-            pltpu.VMEM((4, rows, cols), BF16),
+            pltpu.VMEM((2, rows, cols), BF16),
+            pltpu.VMEM((2, rows, cols), BF16),
             pltpu.VMEM((4, 2, rows, cols), F32),
-            pltpu.VMEM((2, 4, rows, cols), BF16),
-            dma((6,)), dma((3,)), dma((3,)),
+            pltpu.VMEM((2, 2, rows, cols), BF16),
+            pltpu.VMEM((2, rows, cols), BF16),
+            pltpu.VMEM((rows, cols), BF16),
+            pltpu.VMEM((2, rows, cols), BF16),
+            pltpu.VMEM((2, 2, rows, cols), BF16),
+            dma((7,)), dma((3,)), dma((3,)),
             dma((groups, 9)), dma((groups, 9)),
-            dma((groups, 4)), dma((groups, 4)), dma((groups, 4)), dma((groups, 4)),
+            dma((groups, 3)), dma((groups, 3)), dma((groups, 3)), dma((groups, 3)),
+            dma((groups,)), dma((groups,)), dma((groups, 2)), dma((groups, 2)),
             dma((groups, 9)), dma((groups, 9)),
-            dma((groups, 4)), dma((groups, 4)), dma((groups, 4)), dma((groups, 4)),
+            dma((groups, 3)), dma((groups, 3)), dma((groups, 3)), dma((groups, 3)),
+            dma((groups,)), dma((groups,)), dma((groups, 2)), dma((groups, 2)),
         ],
         compiler_params=pltpu.CompilerParams(collective_id=0, has_side_effects=True),
         name="attend_pairs",

time: 61.2 us -> 57.3 us (0.936)
  the two profiles are of different devices: /device:TPU:9 before, /device:TPU:13 now
where the time goes in v1:
time: 57.3 us; the launch traced here: 57.1 us
  Pallas kernels  56.5 us (99%)
  between operations  0.64 us (1%)
    pallas_call x1, Pallas kernels, paired(): pl.pallas_call(functools.partial(fused_kernel, blks, rows, cols), out_sha...  53.8 us
    pallas_call x1, Pallas kernels, paired(): pl.pallas_call(copy_kernel, out_shape=(full,) * 7, in_specs=[vmem] * 7, o...  2.67 us

profile of v1, /device:TPU:13, one launch (start us, length us, event | category | flops | bytes accessed | tf_op | source)
XLA Modules:
  0.0 57.1 jit_solution(17687305565616393650)
XLA Ops:
  0.6 53.8 %attend_pairs.1 = (bf16[128,1024]{1,0:T(8,128)(2,1)}, bf16[128,1024]{1,0:T(8,128)(2,1)}, bf16[128,1024]{1,0:T(8,128)(2,1)}, bf16[128,1024]{1,0:T(8,128)(2,1)}, b...) custom-call(s32[2,8]{1,0:T(2,128)} %off_ref.1, bf16[128,1024]{1,0:T(8,128)(2,1)} %bitcast.14, ...), custom_call_target="tpu_custom_call" | custom-call | tf_op jit(solution)/shard_map/attend_pairs/pallas_call | solution.py:602
  54.4 2.7 %hand_over.1 = (bf16[128,1024]{1,0:T(8,128)(2,1)}, bf16[128,1024]{1,0:T(8,128)(2,1)}, bf16[128,1024]{1,0:T(8,128)(2,1)}, bf16[128,1024]{1,0:T(8,128)(2,1)}, bf16...) custom-call(bf16[128,1024]{1,0:T(8,128)(2,1)} %get-tuple-element.21.refs_0_, ...), custom_call_target="tpu_custom_call" | custom-call | tf_op jit(solution)/shard_map/hand_over/pallas_call | solution.py:637

commit v2 on v1

--- a/solution.py
+++ b/solution.py
@@ -11,7 +11,7 @@
 HEAD = 64
 WINDOW = 2048
 TILE = 512
-LAG = 2
+LAG = 4
 MESH = pl.DeviceIdType.MESH
 F32, BF16 = jnp.float32, jnp.bfloat16
 
@@ -579,8 +579,15 @@
 
 def copy_kernel(*refs):
     count = len(refs) // 2
-    for src, dst in zip(refs[:count], refs[count:]):
-        dst[...] = src[...]
+    sem = refs[-1]
+    copies = [
+        pltpu.make_async_copy(src, dst, sem.at[i])
+        for i, (src, dst) in enumerate(zip(refs[:count], refs[count:-1]))
+    ]
+    for copy in copies:
+        copy.start()
+    for copy in copies:
+        copy.wait()
 
 
 def paired(
@@ -601,7 +608,7 @@
     full = jax.ShapeDtypeStruct((rows, 2 * cols), BF16)
     outs = pl.pallas_call(
         functools.partial(fused_kernel, blks, rows, cols),
-        out_shape=(full,) * 7,
+        out_shape=(pltpu.VMEM((rows, 2 * cols), BF16),) * 7,
         in_specs=[pl.BlockSpec(memory_space=pltpu.SMEM)] + [pl.BlockSpec(memory_space=pl.ANY)] * 8,
         out_specs=(vmem,) * 7,
         scratch_shapes=[
@@ -637,8 +644,10 @@
     outs = pl.pallas_call(
         copy_kernel,
         out_shape=(full,) * 7,
-        in_specs=[vmem] * 7,
-        out_specs=(vmem,) * 7,
+        in_specs=[pl.BlockSpec(memory_space=pl.ANY)] * 7,
+        out_specs=(pl.BlockSpec(memory_space=pl.ANY),) * 7,
+        scratch_shapes=[dma((7,))],
+        compiler_params=pltpu.CompilerParams(vmem_limit_bytes=1 << 20),
         name="hand_over",
     )(*outs)
     return tuple(piece[None] for piece in outs)

time: 57.3 us -> 52.2 us (0.911)
  the two profiles are of different devices: /device:TPU:13 before, /device:TPU:0 now
where the time goes in v2:
time: 52.2 us; the launch traced here: 51.3 us
  Pallas kernels  50.6 us (97%)
  between operations  0.64 us (1%)
    pallas_call x1, Pallas kernels, paired(): pl.pallas_call(functools.partial(fused_kernel, blks, rows, cols), out_sha...  49.3 us
    pallas_call x1, Pallas kernels, paired(): pl.pallas_call(copy_kernel, out_shape=(full,) * 7, in_specs=[pl.BlockSpec...  1.28 us

profile of v2, /device:TPU:0, one launch (start us, length us, event | category | flops | bytes accessed | tf_op | source)
XLA Modules:
  0.0 51.3 jit_solution(4920670465208403034)
XLA Ops:
  0.6 49.3 %attend_pairs.1 = (bf16[128,1024]{1,0:T(8,128)(2,1)S(1)}, bf16[128,1024]{1,0:T(8,128)(2,1)S(1)}, bf16[128,1024]{1,0:T(8,128)(2,1)S(1)}, bf16[128,1024]{1,0:T(8,1...) custom-call(s32[2,8]{1,0:T(2,128)} %off_ref.1, ...), custom_call_target="tpu_custom_call" | custom-call | tf_op jit(solution)/shard_map/attend_pairs/pallas_call | solution.py:609
  50.0 1.3 %hand_over.1 = (bf16[128,1024]{1,0:T(8,128)(2,1)}, bf16[128,1024]{1,0:T(8,128)(2,1)}, bf16[128,1024]{1,0:T(8,128)(2,1)}, bf16[128,1024]{1,0:T(8,128)(2,1)}, bf16...) custom-call(bf16[128,1024]{1,0:T(8,128)(2,1)S(1)} %get-tuple-element.21.refs_0_, ...), custom_call_target="tpu_custom_call" | custom-call | tf_op jit(solution)/shard_map/hand_over/pallas_call | solution.py:644

commit v3 on v0

v3 whole, which is shorter than its diff:
```python
import functools

import jax
import jax.numpy as jnp
from jax import lax
from jax.experimental import pallas as pl
from jax.experimental.pallas import tpu as pltpu
from jax.sharding import PartitionSpec as P

HEADS = 16
HEAD = 64
WINDOW = 2048
TILE = 512
LAG = 4
AHEAD = 5
MESH = pl.DeviceIdType.MESH
F32, BF16 = jnp.float32, jnp.bfloat16


def places():
    tower, blk, seq = lax.axis_index("tower"), lax.axis_index("blk"), lax.axis_index("seq")
    toward = 2 * seq - 1
    peers = dict(
        y=(tower, blk, 1 - seq),
        tower=(1 - tower, blk, seq),
        ahead=(tower, blk + toward, seq),
        behind=(tower, blk - toward, seq),
    )
    return tower, blk, seq, peers


def greet(has_ahead, has_behind, peers):
    barrier = pltpu.get_barrier_semaphore()
    for name in ("y", "tower"):
        pl.semaphore_signal(barrier, inc=1, device_id=peers[name], device_id_type=MESH)
    for name, present in (("ahead", has_ahead), ("behind", has_behind)):
        @pl.when(present)
        def _():
            pl.semaphore_signal(barrier, inc=1, device_id=peers[name], device_id_type=MESH)

    count = 2 + jnp.where(has_ahead, 1, 0) + jnp.where(has_behind, 1, 0)
    pl.semaphore_wait(barrier, count)


def remote(src, dst, send, recv, device):
    return pltpu.make_async_remote_copy(
        src_ref=src, dst_ref=dst, send_sem=send, recv_sem=recv,
        device_id=device, device_id_type=MESH,
    )


def fused_kernel(
    blks, rows, cols,
    off_ref, q_ref, k_ref, v_ref, cq_ref, ck_ref, cv_ref, g_ref, m_ref,
    o_out, gq_out, gk_out, gv_out, gcq_out, gck_out, gcv_out,
    side, pair, halo, partner, far, mate, pick, mask_ext, bias,
    exps, dots, sums, stat, peer_stat,
    mine, y_stage, y_recv, core, x_stage, x_recv, own_stage, own_recv,
    part, mate_part, gpick, gfar,
    local_sem, mask_send, mask_recv, in_send, in_recv, halo_send, halo_recv,
    partner_send, partner_recv, far_send, far_recv, share_send, share_recv,
    stat_send, stat_recv, y_send, y_recv_sem, x_send, x_recv_sem, own_send, own_recv_sem,
    swap_send, swap_recv, gfar_send, gfar_recv, gshare_send, gshare_recv,
):
    tower, blk, seq, peers = places()
    half, wide = rows, 2 * HEAD
    groups = cols // wide
    scale = HEAD ** (-0.5)
    has_low, has_high = blk > 0, blk < blks - 1
    has_ahead = ((seq == 1) & has_high) | ((seq == 0) & has_low)
    has_behind = ((seq == 1) & has_low) | ((seq == 0) & has_high)
    outs = [o_out, gq_out, gcq_out]
    grads = [gk_out, gv_out, gck_out, gcv_out]

    off = off_ref[tower, blk]
    off_ahead = off_ref[tower, jnp.clip(blk + 2 * seq - 1, 0, blks - 1)]
    chosen = jnp.where(seq == 1, jnp.where(off_ahead > 0, 1, 0), jnp.where(off_ahead < 0, 1, 0))
    uses_far = jnp.where(seq == 0, jnp.where(off > 0, 1, 0), jnp.where(off < 0, 1, 0))
    far_from = jnp.where(seq == 0, 0, jnp.where(off < 0, half + off, half))
    far_to = jnp.where(seq == 0, jnp.maximum(off, 0), half)

    def strip(g):
        return pl.ds(pl.multiple_of(g * wide, wide), wide)

    def incoming(g):
        at = strip(g)
        return [
            remote(ref.at[:, at], side.at[i, 1, :, at], in_send.at[g, i], in_recv.at[g, i], peers["y"])
            for i, ref in enumerate((q_ref, cq_ref, g_ref))
        ]

    def haloed(g):
        at = strip(g)
        return [
            remote(
                ref.at[:, at], halo.at[i, :, at], halo_send.at[g, i], halo_recv.at[g, i],
                peers["ahead"],
            )
            for i, ref in enumerate((k_ref, v_ref))
        ]

    def afar(g):
        at = strip(g)
        return remote(
            pick.at[:, at], far.at[tower, :, at], far_send.at[g], far_recv.at[g], peers["ahead"]
        )

    def shared(g):
        at = strip(g)
        return remote(
            far.at[tower, :, at], far.at[tower, :, at], share_send.at[g], share_recv.at[g],
            peers["tower"],
        )

    partners = [
        remote(ref, partner.at[i], partner_send.at[i], partner_recv.at[i], peers["tower"])
        for i, ref in enumerate((ck_ref, cv_ref))
    ]
    mask_ahead = remote(m_ref, mask_ext.at[1], mask_send.at[0], mask_recv.at[0], peers["ahead"])

    def issue(g):
        for copy in incoming(g):
            copy.start()

    def issue_halo(g):
        @pl.when(has_ahead)
        def _():
            for copy in haloed(g):
                copy.start()

    def issue_far(g):
        @pl.when(has_ahead)
        def _():
            afar(g).start()

    locals_ = [
        pltpu.make_async_copy(k_ref, pair.at[0], local_sem.at[0]),
        pltpu.make_async_copy(v_ref, pair.at[1], local_sem.at[1]),
        pltpu.make_async_copy(m_ref, mask_ext.at[0], local_sem.at[2]),
        pltpu.make_async_copy(q_ref, side.at[0, 0], local_sem.at[3]),
        pltpu.make_async_copy(cq_ref, side.at[1, 0], local_sem.at[4]),
        pltpu.make_async_copy(g_ref, side.at[2, 0], local_sem.at[5]),
    ]
    for copy in locals_:
        copy.start()
    for chain, ref in enumerate((ck_ref, cv_ref)):
        @pl.when(tower == chain)
        def _():
            pltpu.make_async_copy(ref, mate, local_sem.at[6]).start()

    @pl.when(jnp.logical_not(has_behind))
    def _():
        halo[...] = jnp.zeros(halo.shape, BF16)
        far[...] = jnp.zeros(far.shape, BF16)
        mask_ext[1] = jnp.zeros(mask_ext.shape[1:], jnp.int32)

    @pl.when(jnp.logical_not(has_ahead))
    def _():
        x_recv[...] = jnp.zeros(x_recv.shape, BF16)
        gfar[...] = jnp.zeros(gfar.shape, BF16)

    for copy in locals_:
        copy.wait()
    for chain, ref in enumerate((ck_ref, cv_ref)):
        @pl.when(tower == chain)
        def _():
            pltpu.make_async_copy(ref, mate, local_sem.at[6]).wait()

    greet(has_ahead, has_behind, peers)

    @pl.when(has_ahead)
    def _():
        mask_ahead.start()

    for copy in partners:
        copy.start()
    first = min(AHEAD, groups)
    for g in range(first):
        issue(g)
    for g in range(min(2, groups)):
        issue_halo(g)
    for copy in partners:
        copy.wait_recv()
    pick[...] = jnp.where(chosen == 1, mate[...], partner[tower])
    for g in range(groups):
        if g >= 2:
            issue_halo(g)
        issue_far(g)

    @pl.when(has_behind)
    def _():
        mask_ahead.wait_recv()

    def column(part_at, chain):
        row = jnp.where(
            chain == 0, mask_ext[part_at, 0:1, :].astype(F32), mask_ext[part_at, 1:2, :].astype(F32)
        )
        return jnp.transpose(jnp.broadcast_to(row, (half, half)))

    row_at = lax.broadcasted_iota(jnp.int32, (half, half), 0)
    col_at = lax.broadcasted_iota(jnp.int32, (half, half), 1)
    apart = (row_at - col_at) * jnp.where(seq == 0, 1, -1)
    from_far = (row_at >= far_from) & (row_at < far_to)
    own_valid, halo_valid = column(0, tower), column(1, tower)
    cross_valid = jnp.where(from_far, column(1, 1 - tower), column(0, 1 - tower))
    allowed = (
        own_valid > 0,
        (own_valid > 0) & (apart >= 0),
        (halo_valid > 0) & (apart <= 0),
        cross_valid > 0,
    )
    for i, near in enumerate(allowed):
        add = jnp.where(near, 0.0, -1e30)
        bias[i, :, :half] = add
        bias[i, :, half:] = add

    lanes = lax.broadcasted_iota(jnp.int32, (half, wide), 1)
    zero = jnp.zeros((half, wide), BF16)

    def split(tile):
        return jnp.concatenate(
            (jnp.where(lanes < HEAD, tile, zero), jnp.where(lanes < HEAD, zero, tile)), 0
        )

    def dot_t(a, b):
        return lax.dot_general(a, b, (((1,), (1,)), ((), ())), preferred_element_type=F32)

    def dot(a, b):
        return jnp.dot(a, b, preferred_element_type=F32)

    def own_heads(both):
        return jnp.concatenate((both[:HEAD, :half], both[HEAD:, half:]), 0)

    def turned(x):
        return jnp.transpose(x.astype(F32)).astype(BF16)

    def operands(g):
        at = strip(g)
        query = [split(side[0, i, :, at] * BF16(scale)) for i in range(2)]
        cross = [split(side[1, i, :, at] * BF16(scale)) for i in range(2)]
        cot = [split(side[2, i, :, at]) for i in range(2)]
        near = [pair[i, :, at] for i in range(2)]
        edge = [halo[i, :, at] for i in range(2)]
        band = [jnp.where(from_far, far[i, :, at], partner[i, :, at]) for i in range(2)]
        return query, cross, cot, near, edge, band

    spans = (slice(0, half), slice(half, 3 * half), slice(3 * half, 4 * half), slice(4 * half, 5 * half))

    def score(g):
        query, cross, cot, near, edge, band = operands(g)
        keys = (near, [jnp.concatenate((n, e), 0) for n, e in zip(near, edge)], band, band)
        asks = (query[0], query[1], cross[0], cross[1])
        adds = (bias[0], jnp.concatenate((bias[1], bias[2]), 0), bias[3], bias[3])
        for kind in range(4):
            key, value = keys[kind]
            scores = dot_t(key, asks[kind]) + adds[kind]
            products = dot_t(value, cot[kind % 2])
            top = jnp.max(scores, axis=0, keepdims=True)
            unnormed = jnp.exp(scores - top)
            total = jnp.sum(unnormed, axis=0, keepdims=True)
            exps[g, spans[kind], :] = unnormed
            dots[g, spans[kind], :] = products
            sums[g, kind : kind + 1, :] = total
            stat[g, 2 * kind : 2 * kind + 1, :] = top + jnp.log(total)
            stat[g, 2 * kind + 1 : 2 * kind + 2, :] = (
                jnp.sum(unnormed * products, axis=0, keepdims=True) / total
            )

    def exchange(g):
        return remote(
            stat.at[g], peer_stat.at[g], stat_send.at[g], stat_recv.at[g], peers["y"]
        )

    def weigh(g, kind):
        other = kind ^ 1
        here, there = stat[g, 2 * kind : 2 * kind + 1, :], peer_stat[g, 2 * other : 2 * other + 1, :]
        top = jnp.maximum(here, there)
        whole = top + jnp.log(jnp.exp(here - top) + jnp.exp(there - top))
        share_here, share_there = jnp.exp(here - whole), jnp.exp(there - whole)
        row_dot = (
            share_here * stat[g, 2 * kind + 1 : 2 * kind + 2, :]
            + share_there * peer_stat[g, 2 * other + 1 : 2 * other + 2, :]
        )
        weights = exps[g, spans[kind], :] * (share_here / sums[g, kind : kind + 1, :])
        grad_scores = weights * (dots[g, spans[kind], :] - row_dot)
        return weights.astype(BF16), grad_scores.astype(BF16)

    def settle(g, swap, relay):
        at = strip(g)
        query, cross, cot, near, edge, band = operands(g)
        band_t = [turned(x) for x in band]
        prob, slope = zip(*[weigh(g, kind) for kind in (2, 3)])
        cross_out = [own_heads(dot(band_t[1], prob[i])) for i in range(2)]
        cross_grad = [own_heads(dot(band_t[0], slope[i])) * scale for i in range(2)]
        band_grad = (
            dot(slope[0], cross[0]) + dot(slope[1], cross[1]),
            dot(prob[0], cot[0]) + dot(prob[1], cot[1]),
        )
        for i in range(2):
            part[i, :, at] = jnp.where(from_far, band_grad[i], 0.0).astype(BF16)
            own_stage[i, :, at] = jnp.where(from_far, 0.0, band_grad[i]).astype(BF16)
        swap()
        near_t = [turned(x) for x in near]
        both_t = [jnp.concatenate((n, turned(e)), 1) for n, e in zip(near_t, edge)]
        prob, slope = zip(*[weigh(g, kind) for kind in (0, 1)])
        self_out = [own_heads(dot(near_t[1], prob[0])), own_heads(dot(both_t[1], prob[1]))]
        self_grad = [own_heads(dot(near_t[0], slope[0])), own_heads(dot(both_t[0], slope[1]))]
        ours = (self_out[0] + cross_out[0], self_grad[0] * scale, cross_grad[0])
        theirs = (self_out[1] + cross_out[1], self_grad[1] * scale, cross_grad[1])
        for i in range(3):
            y_stage[i, :, at] = turned(theirs[i])
            mine[i, :, at] = jnp.transpose(ours[i])
        for i, (left, right, ask) in enumerate(
            ((slope[0], slope[1], query), (prob[0], prob[1], cot))
        ):
            core[i, :, at] = dot(left, ask[0]) + dot(right[:half], ask[1])
            x_stage[i, :, at] = dot(right[half:], ask[1]).astype(BF16)
        relay()

    def outgoing(g):
        at = strip(g)
        return [
            remote(
                y_stage.at[i, :, at], y_recv.at[i, :, at], y_send.at[g, i], y_recv_sem.at[g, i],
                peers["y"],
            )
            for i in range(3)
        ]

    def back(g):
        at = strip(g)
        return [
            remote(
                x_stage.at[i, :, at], x_recv.at[i, :, at], x_send.at[g, i], x_recv_sem.at[g, i],
                peers["behind"],
            )
            for i in range(2)
        ]

    def homeward(g):
        at = strip(g)
        return [
            remote(
                own_stage.at[i, :, at], own_recv.at[i, :, at],
                own_send.at[g, i], own_recv_sem.at[g, i], peers["tower"],
            )
            for i in range(2)
        ]

    def swapped_part(g):
        at = strip(g)
        return remote(
            part.at[1 - tower, :, at], mate_part.at[:, at], swap_send.at[g], swap_recv.at[g],
            peers["tower"],
        )

    def far_back(g):
        at = strip(g)
        return remote(
            gpick.at[:, at], gfar.at[tower, :, at], gfar_send.at[g], gfar_recv.at[g],
            peers["behind"],
        )

    def gshared(g):
        at = strip(g)
        return remote(
            gfar.at[tower, :, at], gfar.at[tower, :, at], gshare_send.at[g], gshare_recv.at[g],
            peers["tower"],
        )

    def share(g):
        @pl.when(has_behind)
        def _():
            afar(g).wait_recv()
            shared(g).start()

    def compute(g):
        def swap():
            swapped_part(g).start()
            for copy in homeward(g):
                copy.start()

        def relay():
            at = strip(g)
            for copy in outgoing(g):
                copy.start()
            swapped_part(g).wait_recv()
            gpick[:, at] = jnp.where(uses_far == 1, part[tower, :, at], mate_part[:, at])

            @pl.when(has_behind)
            def _():
                far_back(g).start()
                for copy in back(g):
                    copy.start()

        settle(g, swap, relay)

    def finish(g):
        at = strip(g)

        @pl.when(has_ahead)
        def _():
            far_back(g).wait_recv()
            gshared(g).start()
            for copy in back(g):
                copy.wait_recv()

        for i in range(2):
            grads[i][:, at] = (core[i, :, at] + x_recv[i, :, at].astype(F32)).astype(BF16)
        for i, copy in enumerate(outgoing(g)):
            copy.wait_recv()
            outs[i][:, at] = (mine[i, :, at] + y_recv[i, :, at].astype(F32)).astype(BF16)

        @pl.when(has_ahead)
        def _():
            gshared(g).wait_recv()

        for i, copy in enumerate(homeward(g)):
            copy.wait_recv()
            more = jnp.where(chosen == 1, gfar[i, :, at].astype(F32), 0.0)
            grads[2 + i][:, at] = (own_recv[i, :, at].astype(F32) + more).astype(BF16)

    def step(g, carry):
        @pl.when(g + AHEAD < groups)
        def _():
            issue(g + AHEAD)

        @pl.when(g < groups)
        def _():
            for copy in incoming(g):
                copy.wait_recv()

            @pl.when(has_behind)
            def _():
                for copy in haloed(g):
                    copy.wait_recv()
                shared(g).wait_recv()

            score(g)
            exchange(g).start()

        @pl.when(g + 1 < groups)
        def _():
            share(g + 1)

        @pl.when(g >= LAG)
        def _():
            exchange(g - LAG).wait_recv()
            compute(g - LAG)

        return carry

    share(0)
    lax.fori_loop(0, groups + LAG, step, 0)

    def end(g, carry):
        finish(g)
        return carry

    lax.fori_loop(0, groups, end, 0)

    def close(g, carry):
        for copy in incoming(g) + outgoing(g) + homeward(g):
            copy.wait_send()
        exchange(g).wait_send()
        swapped_part(g).wait_send()

        @pl.when(has_ahead)
        def _():
            for copy in haloed(g):
                copy.wait_send()
            afar(g).wait_send()
            gshared(g).wait_send()

        @pl.when(has_behind)
        def _():
            shared(g).wait_send()
            far_back(g).wait_send()
            for copy in back(g):
                copy.wait_send()

        return carry

    lax.fori_loop(0, groups, close, 0)
    for copy in partners:
        copy.wait_send()

    @pl.when(has_ahead)
    def _():
        mask_ahead.wait_send()


def copy_kernel(*refs):
    count = len(refs) // 2
    sem = refs[-1]
    copies = [
        pltpu.make_async_copy(src, dst, sem.at[i])
        for i, (src, dst) in enumerate(zip(refs[:count], refs[count:-1]))
    ]
    for copy in copies:
        copy.start()
    for copy in copies:
        copy.wait()


def paired(
    queries, key_rows, value_rows, cross_queries, cross_keys, cross_values, grad_out,
    offsets, key_valid,
):
    blks = lax.axis_size("blk")
    values = [
        value[0] for value in (
            queries, key_rows, value_rows, cross_queries, cross_keys, cross_values, grad_out
        )
    ]
    rows, cols = queries.shape[1:]
    groups, wide = cols // (2 * HEAD), 2 * rows
    dma = pltpu.SemaphoreType.DMA
    full = jax.ShapeDtypeStruct((rows, cols), BF16)
    narrow = pltpu.VMEM((2, rows, cols), BF16)
    single = pltpu.VMEM((rows, cols), BF16)
    scored = pltpu.VMEM((groups, 5 * rows, wide), F32)
    stats = pltpu.VMEM((groups, 8, wide), F32)
    pairs = (dma((groups, 2)),) * 2
    ones = (dma((groups,)),) * 2
    outs = pl.pallas_call(
        functools.partial(fused_kernel, blks, rows, cols),
        out_shape=(pltpu.VMEM((rows, cols), BF16),) * 7,
        in_specs=[pl.BlockSpec(memory_space=pltpu.SMEM)] + [pl.BlockSpec(memory_space=pl.ANY)] * 8,
        out_specs=(pl.BlockSpec(memory_space=pltpu.VMEM),) * 7,
        scratch_shapes=[
            pltpu.VMEM((3, 2, rows, cols), BF16),
            narrow, narrow, narrow, narrow, single, single,
            pltpu.VMEM((2,) + key_valid.shape, jnp.int32),
            pltpu.VMEM((4, rows, wide), F32),
            scored, scored, stats, stats, stats,
            pltpu.VMEM((3, rows, cols), F32),
            pltpu.VMEM((3, rows, cols), BF16), pltpu.VMEM((3, rows, cols), BF16),
            pltpu.VMEM((2, rows, cols), F32),
            narrow, narrow, narrow, narrow, narrow, single, single, narrow,
            dma((7,)), dma((1,)), dma((1,)),
            dma((groups, 3)), dma((groups, 3)), *pairs,
            dma((2,)), dma((2,)), *ones, *ones,
            *ones, dma((groups, 3)), dma((groups, 3)), *pairs, *pairs,
            *ones, *ones, *ones,
        ],
        compiler_params=pltpu.CompilerParams(collective_id=0, has_side_effects=True),
        name="attend_pairs",
    )(offsets, *values, key_valid)
    outs = pl.pallas_call(
        copy_kernel,
        out_shape=(full,) * 7,
        in_specs=[pl.BlockSpec(memory_space=pl.ANY)] * 7,
        out_specs=(pl.BlockSpec(memory_space=pl.ANY),) * 7,
        scratch_shapes=[dma((7,))],
        compiler_params=pltpu.CompilerParams(vmem_limit_bytes=1 << 20),
        name="hand_over",
    )(*outs)
    return tuple(piece[None] for piece in outs)


def extended(block, sides, width):
    for axis, dim in sides:
        count = lax.axis_size(axis)
        forward = [(i, i + 1) for i in range(count - 1)]
        backward = [(target, source) for source, target in forward]
        low = lax.ppermute(
            lax.slice_in_dim(block, block.shape[dim] - width, None, axis=dim), axis, forward
        )
        high = lax.ppermute(lax.slice_in_dim(block, 0, width, axis=dim), axis, backward)
        block = jnp.concatenate([low, block, high], axis=dim)
    return block


def swapped(value, axis, bit):
    mask = 2**bit
    pairs = [(source, source ^ mask) for source in range(lax.axis_size(axis))]
    return lax.ppermute(value, axis, pairs)


def passed_along(block, axis, distance):
    devices = range(lax.axis_size(axis))
    route = [(i - distance, i) for i in devices if i - distance in devices]
    return lax.ppermute(block, axis, route)


def attend(query_tile, grad_tile, key_block, value_block, allowed, heads_here):
    score_scale = HEAD ** (-0.5)
    rows_count = query_tile.shape[0]
    keys_count = key_block.shape[0]
    q_heads = query_tile.reshape(rows_count, heads_here, HEAD)
    g_heads = grad_tile.reshape(rows_count, heads_here, HEAD)
    k_heads = key_block.reshape(keys_count, heads_here, HEAD)
    v_heads = value_block.reshape(keys_count, heads_here, HEAD)
    scores = (
        jnp.einsum("qhe,khe->hqk", q_heads, k_heads, preferred_element_type=jnp.float32)
        * score_scale
    )
    scores = jnp.where(allowed[None], scores, -1e30)
    row_max = jnp.max(scores, axis=2)
    unnormed = jnp.exp(scores - row_max[:, :, None])
    row_sum = jnp.sum(unnormed, axis=2)
    weights = unnormed / row_sum[:, :, None]
    prob_bf = weights.astype(jnp.bfloat16)
    result = jnp.einsum(
        "hqk,khe->qhe", prob_bf, v_heads, preferred_element_type=jnp.float32
    ).reshape(rows_count, -1)
    grad_probs = jnp.einsum("qhe,khe->hqk", g_heads, v_heads, preferred_element_type=jnp.float32)
    row_dot = jnp.sum(weights * grad_probs, axis=2)
    grad_scores = (weights * (grad_probs - row_dot[:, :, None]) * score_scale).astype(jnp.bfloat16)
    grad_query = jnp.einsum(
        "hqk,khe->qhe", grad_scores, k_heads, preferred_element_type=jnp.float32
    ).reshape(rows_count, -1)
    grad_key = jnp.einsum(
        "hqk,qhe->khe", grad_scores, q_heads, preferred_element_type=jnp.float32
    ).reshape(keys_count, -1)
    grad_value = jnp.einsum(
        "hqk,qhe->khe", prob_bf, g_heads, preferred_element_type=jnp.float32
    ).reshape(keys_count, -1)
    return (result, grad_query, grad_key, grad_value, jnp.stack((row_max, row_sum, row_dot)))


def shards(
    queries,
    key_rows,
    value_rows,
    cross_queries,
    cross_keys,
    cross_values,
    grad_out,
    offsets,
    key_valid,
):
    seq_count = lax.axis_size("seq")
    heads_here = HEADS // seq_count
    local_rows = (
        queries[0],
        key_rows[0],
        value_rows[0],
        cross_queries[0],
        cross_keys[0],
        cross_values[0],
        grad_out[0],
    )
    query_here, key_here, value_here, cross_query, cross_key, cross_value, cotangent = (
        lax.all_to_all(local_rows[0], "seq", split_axis=1, concat_axis=0, tiled=True),
        lax.all_to_all(local_rows[1], "seq", split_axis=1, concat_axis=0, tiled=True),
        lax.all_to_all(local_rows[2], "seq", split_axis=1, concat_axis=0, tiled=True),
        lax.all_to_all(local_rows[3], "seq", split_axis=1, concat_axis=0, tiled=True),
        lax.all_to_all(local_rows[4], "seq", split_axis=1, concat_axis=0, tiled=True),
        lax.all_to_all(local_rows[5], "seq", split_axis=1, concat_axis=0, tiled=True),
        lax.all_to_all(local_rows[6], "seq", split_axis=1, concat_axis=0, tiled=True),
    )
    block_len = query_here.shape[0]
    columns = query_here.shape[1]
    half_width = min(WINDOW // 2, block_len // 2)
    tile_rows = min(TILE, block_len)
    tile_count = block_len // tile_rows
    window_span = tile_rows + 2 * half_width
    tower_id = lax.axis_index("tower")
    block_id = lax.axis_index("blk")
    block_mask = lax.all_gather(key_valid, "seq", axis=1, tiled=True)
    mask_ext = extended(block_mask, (("blk", 1),), half_width)
    self_valid = lax.dynamic_index_in_dim(mask_ext, tower_id, 0, keepdims=False)
    other_valid = lax.dynamic_index_in_dim(mask_ext, 1 - tower_id, 0, keepdims=False)
    pair_ext = extended(jnp.stack((key_here, value_here)), (("blk", 1),), half_width)
    partner = swapped(jnp.stack((cross_key, cross_value)), "tower", 0)
    partner_ext = extended(partner, (("blk", 1),), half_width)
    align_shift = offsets[tower_id, block_id]
    band_start = half_width + align_shift
    band = lax.dynamic_slice_in_dim(partner_ext, band_start, block_len, 1)
    band_valid = lax.dynamic_slice_in_dim(other_valid, band_start, block_len) > 0
    rows_local = jnp.arange(tile_rows)
    keys_local = jnp.arange(window_span)
    near = jnp.abs(rows_local[:, None] + half_width - keys_local[None, :]) <= half_width

    def self_step(carry, tile_index):
        grad_key_acc, grad_value_acc = carry
        tile_start = tile_index * tile_rows
        query_tile = lax.dynamic_slice_in_dim(query_here, tile_start, tile_rows, 0)
        grad_tile = lax.dynamic_slice_in_dim(cotangent, tile_start, tile_rows, 0)
        key_window = lax.dynamic_slice_in_dim(pair_ext[0], tile_start, window_span, 0)
        value_window = lax.dynamic_slice_in_dim(pair_ext[1], tile_start, window_span, 0)
        allowed = (
            near & (lax.dynamic_slice_in_dim(self_valid, tile_start, window_span) > 0)[None, :]
        )
        result, grad_query, grad_key, grad_value, stats = attend(
            query_tile, grad_tile, key_window, value_window, allowed, heads_here
        )
        grad_key_acc = lax.dynamic_update_slice_in_dim(
            grad_key_acc,
            lax.dynamic_slice_in_dim(grad_key_acc, tile_start, window_span, 0) + grad_key,
            tile_start,
            0,
        )
        grad_value_acc = lax.dynamic_update_slice_in_dim(
            grad_value_acc,
            lax.dynamic_slice_in_dim(grad_value_acc, tile_start, window_span, 0) + grad_value,
            tile_start,
            0,
        )
        return ((grad_key_acc, grad_value_acc), (result, grad_query, stats))

    def cross_step(carry, tile_index):
        grad_key_acc, grad_value_acc = carry
        tile_start = tile_index * tile_rows
        query_tile = lax.dynamic_slice_in_dim(cross_query, tile_start, tile_rows, 0)
        grad_tile = lax.dynamic_slice_in_dim(cotangent, tile_start, tile_rows, 0)
        result, grad_query, grad_key, grad_value, stats = attend(
            query_tile, grad_tile, band[0], band[1], band_valid[None, :], heads_here
        )
        return ((grad_key_acc + grad_key, grad_value_acc + grad_value), (result, grad_query))

    zeros_ext = jnp.zeros((block_len + 2 * half_width, columns), jnp.float32)
    zeros_band = jnp.zeros((block_len, columns), jnp.float32)
    tile_ids = jnp.arange(tile_count)
    (self_gk, self_gv), (self_out, self_gq, self_stats) = lax.scan(
        self_step, (zeros_ext, zeros_ext), tile_ids
    )
    (cross_gk, cross_gv), (cross_out, cross_gq) = lax.scan(
        cross_step, (zeros_band, zeros_band), tile_ids
    )
    self_out = self_out.reshape(block_len, columns)
    cross_out = cross_out.reshape(block_len, columns)
    self_stats = jnp.transpose(self_stats, (1, 2, 0, 3)).reshape(3, heads_here, block_len)
    attended = (self_out + cross_out).astype(jnp.bfloat16)
    cross_ext = jnp.zeros((2, block_len + 2 * half_width, columns), jnp.float32)
    cross_ext = lax.dynamic_update_slice_in_dim(
        cross_ext, jnp.stack((cross_gk, cross_gv)), band_start, 1
    )
    self_ext = jnp.stack((self_gk, self_gv))
    self_core = self_ext[:, half_width : half_width + block_len]
    cross_core = cross_ext[:, half_width : half_width + block_len]
    upper_cut = block_len - half_width
    lower_send = jnp.concatenate((self_ext[:, :half_width], cross_ext[:, :half_width]), 0)
    upper_send = jnp.concatenate(
        (self_ext[:, block_len + half_width :], cross_ext[:, block_len + half_width :]), 0
    )
    from_above = passed_along(lower_send.astype(jnp.bfloat16), "blk", -1).astype(lower_send.dtype)
    from_below = passed_along(upper_send.astype(jnp.bfloat16), "blk", 1).astype(upper_send.dtype)
    self_core = (
        self_core.at[:, upper_cut:].add(from_above[:2]).at[:, :half_width].add(from_below[:2])
    )
    cross_core = (
        cross_core.at[:, upper_cut:].add(from_above[2:]).at[:, :half_width].add(from_below[2:])
    )
    returned = swapped(cross_core.astype(jnp.bfloat16), "tower", 0)
    head_outs = (
        attended,
        self_gq.reshape(block_len, columns).astype(jnp.bfloat16),
        self_core[0].astype(jnp.bfloat16),
        self_core[1].astype(jnp.bfloat16),
        cross_gq.reshape(block_len, columns).astype(jnp.bfloat16),
        returned[0],
        returned[1],
    )
    token_outs = (
        lax.all_to_all(head_outs[0], "seq", split_axis=0, concat_axis=1, tiled=True),
        lax.all_to_all(head_outs[1], "seq", split_axis=0, concat_axis=1, tiled=True),
        lax.all_to_all(head_outs[2], "seq", split_axis=0, concat_axis=1, tiled=True),
        lax.all_to_all(head_outs[3], "seq", split_axis=0, concat_axis=1, tiled=True),
        lax.all_to_all(head_outs[4], "seq", split_axis=0, concat_axis=1, tiled=True),
        lax.all_to_all(head_outs[5], "seq", split_axis=0, concat_axis=1, tiled=True),
        lax.all_to_all(head_outs[6], "seq", split_axis=0, concat_axis=1, tiled=True),
    )
    return tuple((piece[None] for piece in token_outs))


def solution(mesh):
    in_specs = (
        P("tower", ("blk", "seq"), None),
        P("tower", ("blk", "seq"), None),
        P("tower", ("blk", "seq"), None),
        P("tower", ("blk", "seq"), None),
        P("tower", ("blk", "seq"), None),
        P("tower", ("blk", "seq"), None),
        P("tower", ("blk", "seq"), None),
        P(),
        P(None, ("blk", "seq")),
    )
    out_specs = (
        P("tower", ("blk", "seq"), None),
        P("tower", ("blk", "seq"), None),
        P("tower", ("blk", "seq"), None),
        P("tower", ("blk", "seq"), None),
        P("tower", ("blk", "seq"), None),
        P("tower", ("blk", "seq"), None),
        P("tower", ("blk", "seq"), None),
    )
    body = paired if mesh.shape["seq"] == 2 else shards
    return jax.shard_map(body, mesh=mesh, in_specs=in_specs, out_specs=out_specs, check_vma=False)
```

time: 61.2 us -> 47.3 us (0.77)
  the two profiles are of different devices: /device:TPU:9 before, /device:TPU:0 now
where the time goes in v3:
time: 47.3 us; the launch traced here: 47.2 us
  Pallas kernels  46.5 us (98%)
  between operations  0.64 us (1%)
    pallas_call x1, Pallas kernels, paired(): pl.pallas_call(functools.partial(fused_kernel, blks, rows, cols), out_sha...  45.2 us
    pallas_call x1, Pallas kernels, paired(): pl.pallas_call(copy_kernel, out_shape=(full,) * 7, in_specs=[pl.BlockSpec...  1.28 us

profile of v3, /device:TPU:0, one launch (start us, length us, event | category | flops | bytes accessed | tf_op | source)
XLA Modules:
  0.0 47.2 jit_solution(17918154473093518548)
XLA Ops:
  0.6 45.2 %attend_pairs.1 = (bf16[128,1024]{1,0:T(8,128)(2,1)S(1)}, bf16[128,1024]{1,0:T(8,128)(2,1)S(1)}, bf16[128,1024]{1,0:T(8,128)(2,1)S(1)}, bf16[128,1024]{1,0:T(8,1...) custom-call(s32[2,8]{1,0:T(2,128)} %off_ref.1, ...), custom_call_target="tpu_custom_call" | custom-call | tf_op jit(solution)/shard_map/attend_pairs/pallas_call | solution.py:526
  45.9 1.3 %hand_over.1 = (bf16[128,1024]{1,0:T(8,128)(2,1)}, bf16[128,1024]{1,0:T(8,128)(2,1)}, bf16[128,1024]{1,0:T(8,128)(2,1)}, bf16[128,1024]{1,0:T(8,128)(2,1)}, bf16...) custom-call(bf16[128,1024]{1,0:T(8,128)(2,1)S(1)} %get-tuple-element.21.refs_0_, ...), custom_call_target="tpu_custom_call" | custom-call | tf_op jit(solution)/shard_map/hand_over/pallas_call | solution.py:550

commit v4 on v3

--- a/solution.py
+++ b/solution.py
@@ -38,8 +38,10 @@
         def _():
             pl.semaphore_signal(barrier, inc=1, device_id=peers[name], device_id_type=MESH)
 
+
+def meet(has_ahead, has_behind):
     count = 2 + jnp.where(has_ahead, 1, 0) + jnp.where(has_behind, 1, 0)
-    pl.semaphore_wait(barrier, count)
+    pl.semaphore_wait(pltpu.get_barrier_semaphore(), count)
 
 
 def remote(src, dst, send, recv, device):
@@ -133,6 +135,7 @@
         def _():
             afar(g).start()
 
+    greet(has_ahead, has_behind, peers)
     locals_ = [
         pltpu.make_async_copy(k_ref, pair.at[0], local_sem.at[0]),
         pltpu.make_async_copy(v_ref, pair.at[1], local_sem.at[1]),
@@ -159,26 +162,26 @@
         x_recv[...] = jnp.zeros(x_recv.shape, BF16)
         gfar[...] = jnp.zeros(gfar.shape, BF16)
 
+    meet(has_ahead, has_behind)
+    first = min(AHEAD, groups)
+    issue(0)
+
+    @pl.when(has_ahead)
+    def _():
+        mask_ahead.start()
+
+    for copy in partners:
+        copy.start()
+    for g in range(1, first):
+        issue(g)
+    for g in range(min(2, groups)):
+        issue_halo(g)
     for copy in locals_:
         copy.wait()
     for chain, ref in enumerate((ck_ref, cv_ref)):
         @pl.when(tower == chain)
         def _():
             pltpu.make_async_copy(ref, mate, local_sem.at[6]).wait()
-
-    greet(has_ahead, has_behind, peers)
-
-    @pl.when(has_ahead)
-    def _():
-        mask_ahead.start()
-
-    for copy in partners:
-        copy.start()
-    first = min(AHEAD, groups)
-    for g in range(first):
-        issue(g)
-    for g in range(min(2, groups)):
-        issue_halo(g)
     for copy in partners:
         copy.wait_recv()
     pick[...] = jnp.where(chosen == 1, mate[...], partner[tower])
@@ -455,11 +458,6 @@
 
     def end(g, carry):
         finish(g)
-        return carry
-
-    lax.fori_loop(0, groups, end, 0)
-
-    def close(g, carry):
         for copy in incoming(g) + outgoing(g) + homeward(g):
             copy.wait_send()
         exchange(g).wait_send()
@@ -481,13 +479,14 @@
 
         return carry
 
-    lax.fori_loop(0, groups, close, 0)
     for copy in partners:
         copy.wait_send()
 
     @pl.when(has_ahead)
     def _():
         mask_ahead.wait_send()
+
+    lax.fori_loop(0, groups, end, 0)
 
 
 def copy_kernel(*refs):

time: 47.3 us -> 45.8 us (0.968)
  Pallas kernels: 46.5 us -> 45 us
    pallas_call x1, Pallas kernels: 45.2 us -> 43.8 us  [paired(): pl.pallas_call(functools.partial(fused_kernel, blks, rows, cols), out_sha...]
where the time goes in v4:
time: 45.8 us; the launch traced here: 45.7 us
  Pallas kernels  45 us (98%)
  between operations  0.64 us (1%)
    pallas_call x1, Pallas kernels, paired(): pl.pallas_call(functools.partial(fused_kernel, blks, rows, cols), out_sha...  43.8 us
    pallas_call x1, Pallas kernels, paired(): pl.pallas_call(copy_kernel, out_shape=(full,) * 7, in_specs=[pl.BlockSpec...  1.28 us

profile of v4, /device:TPU:0, one launch (start us, length us, event | category | flops | bytes accessed | tf_op | source)
XLA Modules:
  0.0 45.7 jit_solution(2126152195494330209)
XLA Ops:
  0.6 43.8 %attend_pairs.1 = (bf16[128,1024]{1,0:T(8,128)(2,1)S(1)}, bf16[128,1024]{1,0:T(8,128)(2,1)S(1)}, bf16[128,1024]{1,0:T(8,128)(2,1)S(1)}, bf16[128,1024]{1,0:T(8,1...) custom-call(s32[2,8]{1,0:T(2,128)} %off_ref.1, ...), custom_call_target="tpu_custom_call" | custom-call | tf_op jit(solution)/shard_map/attend_pairs/pallas_call | solution.py:525
  44.4 1.3 %hand_over.1 = (bf16[128,1024]{1,0:T(8,128)(2,1)}, bf16[128,1024]{1,0:T(8,128)(2,1)}, bf16[128,1024]{1,0:T(8,128)(2,1)}, bf16[128,1024]{1,0:T(8,128)(2,1)}, bf16...) custom-call(bf16[128,1024]{1,0:T(8,128)(2,1)S(1)} %get-tuple-element.21.refs_0_, ...), custom_call_target="tpu_custom_call" | custom-call | tf_op jit(solution)/shard_map/hand_over/pallas_call | solution.py:549

commit v5 on v4

--- a/solution.py
+++ b/solution.py
@@ -53,9 +53,9 @@
 
 def fused_kernel(
     blks, rows, cols,
-    off_ref, q_ref, k_ref, v_ref, cq_ref, ck_ref, cv_ref, g_ref, m_ref,
+    offsets_ref, q_ref, k_ref, v_ref, cq_ref, ck_ref, cv_ref, g_ref, m_ref,
     o_out, gq_out, gk_out, gv_out, gcq_out, gck_out, gcv_out,
-    side, pair, halo, partner, far, mate, pick, mask_ext, bias,
+    off_ref, side, pair, halo, partner, far, mate, pick, mask_ext, bias,
     exps, dots, sums, stat, peer_stat,
     mine, y_stage, y_recv, core, x_stage, x_recv, own_stage, own_recv,
     part, mate_part, gpick, gfar,
@@ -74,13 +74,6 @@
     outs = [o_out, gq_out, gcq_out]
     grads = [gk_out, gv_out, gck_out, gcv_out]
 
-    off = off_ref[tower, blk]
-    off_ahead = off_ref[tower, jnp.clip(blk + 2 * seq - 1, 0, blks - 1)]
-    chosen = jnp.where(seq == 1, jnp.where(off_ahead > 0, 1, 0), jnp.where(off_ahead < 0, 1, 0))
-    uses_far = jnp.where(seq == 0, jnp.where(off > 0, 1, 0), jnp.where(off < 0, 1, 0))
-    far_from = jnp.where(seq == 0, 0, jnp.where(off < 0, half + off, half))
-    far_to = jnp.where(seq == 0, jnp.maximum(off, 0), half)
-
     def strip(g):
         return pl.ds(pl.multiple_of(g * wide, wide), wide)
 
@@ -137,6 +130,7 @@
 
     greet(has_ahead, has_behind, peers)
     locals_ = [
+        pltpu.make_async_copy(offsets_ref, off_ref, local_sem.at[7]),
         pltpu.make_async_copy(k_ref, pair.at[0], local_sem.at[0]),
         pltpu.make_async_copy(v_ref, pair.at[1], local_sem.at[1]),
         pltpu.make_async_copy(m_ref, mask_ext.at[0], local_sem.at[2]),
@@ -182,6 +176,13 @@
         @pl.when(tower == chain)
         def _():
             pltpu.make_async_copy(ref, mate, local_sem.at[6]).wait()
+    off = off_ref[tower, blk]
+    off_ahead = off_ref[tower, jnp.clip(blk + 2 * seq - 1, 0, blks - 1)]
+    chosen = jnp.where(seq == 1, jnp.where(off_ahead > 0, 1, 0), jnp.where(off_ahead < 0, 1, 0))
+    uses_far = jnp.where(seq == 0, jnp.where(off > 0, 1, 0), jnp.where(off < 0, 1, 0))
+    far_from = jnp.where(seq == 0, 0, jnp.where(off < 0, half + off, half))
+    far_to = jnp.where(seq == 0, jnp.maximum(off, 0), half)
+
     for copy in partners:
         copy.wait_recv()
     pick[...] = jnp.where(chosen == 1, mate[...], partner[tower])
@@ -525,9 +526,10 @@
     outs = pl.pallas_call(
         functools.partial(fused_kernel, blks, rows, cols),
         out_shape=(pltpu.VMEM((rows, cols), BF16),) * 7,
-        in_specs=[pl.BlockSpec(memory_space=pltpu.SMEM)] + [pl.BlockSpec(memory_space=pl.ANY)] * 8,
+        in_specs=[pl.BlockSpec(memory_space=pl.ANY)] * 9,
         out_specs=(pl.BlockSpec(memory_space=pltpu.VMEM),) * 7,
         scratch_shapes=[
+            pltpu.SMEM(offsets.shape, jnp.int32),
             pltpu.VMEM((3, 2, rows, cols), BF16),
             narrow, narrow, narrow, narrow, single, single,
             pltpu.VMEM((2,) + key_valid.shape, jnp.int32),
@@ -537,7 +539,7 @@
             pltpu.VMEM((3, rows, cols), BF16), pltpu.VMEM((3, rows, cols), BF16),
             pltpu.VMEM((2, rows, cols), F32),
             narrow, narrow, narrow, narrow, narrow, single, single, narrow,
-            dma((7,)), dma((1,)), dma((1,)),
+            dma((8,)), dma((1,)), dma((1,)),
             dma((groups, 3)), dma((groups, 3)), *pairs,
             dma((2,)), dma((2,)), *ones, *ones,
             *ones, dma((groups, 3)), dma((groups, 3)), *pairs, *pairs,

time: 45.8 us -> 45.1 us (0.985)
  Pallas kernels: 45 us -> 44.4 us
    pallas_call x1, Pallas kernels: 43.8 us -> 43.1 us  [paired(): pl.pallas_call(functools.partial(fused_kernel, blks, rows, cols), out_sha...]
where the time goes in v5:
time: 45.1 us; the launch traced here: 45 us
  Pallas kernels  44.4 us (98%)
  between operations  0.64 us (1%)
    pallas_call x1, Pallas kernels, paired(): pl.pallas_call(functools.partial(fused_kernel, blks, rows, cols), out_sha...  43.1 us
    pallas_call x1, Pallas kernels, paired(): pl.pallas_call(copy_kernel, out_shape=(full,) * 7, in_specs=[pl.BlockSpec...  1.28 us

profile of v5, /device:TPU:0, one launch (start us, length us, event | category | flops | bytes accessed | tf_op | source)
XLA Modules:
  0.0 45.0 jit_solution(16350483296989272521)
XLA Ops:
  0.6 43.1 %attend_pairs.1 = (bf16[128,1024]{1,0:T(8,128)(2,1)S(1)}, bf16[128,1024]{1,0:T(8,128)(2,1)S(1)}, bf16[128,1024]{1,0:T(8,128)(2,1)S(1)}, bf16[128,1024]{1,0:T(8,1...) custom-call(s32[2,8]{1,0:T(2,128)} %offsets_ref.1, ...), custom_call_target="tpu_custom_call" | custom-call | tf_op jit(solution)/shard_map/attend_pairs/pallas_call | solution.py:526
  43.7 1.3 %hand_over.1 = (bf16[128,1024]{1,0:T(8,128)(2,1)}, bf16[128,1024]{1,0:T(8,128)(2,1)}, bf16[128,1024]{1,0:T(8,128)(2,1)}, bf16[128,1024]{1,0:T(8,128)(2,1)}, bf16...) custom-call(bf16[128,1024]{1,0:T(8,128)(2,1)S(1)} %get-tuple-element.21.refs_0_, ...), custom_call_target="tpu_custom_call" | custom-call | tf_op jit(solution)/shard_map/hand_over/pallas_call | solution.py:551

commit v6 on v5

--- a/solution.py
+++ b/solution.py
@@ -56,7 +56,7 @@
     offsets_ref, q_ref, k_ref, v_ref, cq_ref, ck_ref, cv_ref, g_ref, m_ref,
     o_out, gq_out, gk_out, gv_out, gcq_out, gck_out, gcv_out,
     off_ref, side, pair, halo, partner, far, mate, pick, mask_ext, bias,
-    exps, dots, sums, stat, peer_stat,
+    exps, dots, sums, stat, flat, packed, peer_packed,
     mine, y_stage, y_recv, core, x_stage, x_recv, own_stage, own_recv,
     part, mate_part, gpick, gfar,
     local_sem, mask_send, mask_recv, in_send, in_recv, halo_send, halo_recv,
@@ -265,25 +265,41 @@
             exps[g, spans[kind], :] = unnormed
             dots[g, spans[kind], :] = products
             sums[g, kind : kind + 1, :] = total
-            stat[g, 2 * kind : 2 * kind + 1, :] = top + jnp.log(total)
-            stat[g, 2 * kind + 1 : 2 * kind + 2, :] = (
-                jnp.sum(unnormed * products, axis=0, keepdims=True) / total
-            )
+            merged = top + jnp.log(total)
+            row_dot = jnp.sum(unnormed * products, axis=0, keepdims=True) / total
+            stat[g, 2 * kind : 2 * kind + 1, :] = merged
+            stat[g, 2 * kind + 1 : 2 * kind + 2, :] = row_dot
+            for head in range(2):
+                lane = slice(head * half, (head + 1) * half)
+                at = 2 * kind + head
+                flat[0, at : at + 1, :] = merged[:, lane]
+                flat[1, at : at + 1, :] = row_dot[:, lane]
+        high = flat[0].astype(BF16)
+        low = (flat[0] - high.astype(F32)).astype(BF16)
+        packed[g] = jnp.concatenate((high, low, flat[1].astype(BF16)), 1)
 
     def exchange(g):
         return remote(
-            stat.at[g], peer_stat.at[g], stat_send.at[g], stat_recv.at[g], peers["y"]
+            packed.at[g], peer_packed.at[g], stat_send.at[g], stat_recv.at[g], peers["y"]
         )
 
     def weigh(g, kind):
-        other = kind ^ 1
-        here, there = stat[g, 2 * kind : 2 * kind + 1, :], peer_stat[g, 2 * other : 2 * other + 1, :]
+        peer = peer_packed[g].astype(F32)
+        at = 2 * (kind ^ 1)
+
+        def joined(rows_of):
+            return jnp.concatenate((rows_of[at : at + 1], rows_of[at + 1 : at + 2]), 1)
+
+        here, there = (
+            stat[g, 2 * kind : 2 * kind + 1, :],
+            joined(peer[:, :half] + peer[:, half : 2 * half]),
+        )
         top = jnp.maximum(here, there)
         whole = top + jnp.log(jnp.exp(here - top) + jnp.exp(there - top))
         share_here, share_there = jnp.exp(here - whole), jnp.exp(there - whole)
         row_dot = (
             share_here * stat[g, 2 * kind + 1 : 2 * kind + 2, :]
-            + share_there * peer_stat[g, 2 * other + 1 : 2 * other + 2, :]
+            + share_there * joined(peer[:, 2 * half :])
         )
         weights = exps[g, spans[kind], :] * (share_here / sums[g, kind : kind + 1, :])
         grad_scores = weights * (dots[g, spans[kind], :] - row_dot)
@@ -521,6 +537,7 @@
     single = pltpu.VMEM((rows, cols), BF16)
     scored = pltpu.VMEM((groups, 5 * rows, wide), F32)
     stats = pltpu.VMEM((groups, 8, wide), F32)
+    bits = pltpu.VMEM((groups, 8, 3 * rows), BF16)
     pairs = (dma((groups, 2)),) * 2
     ones = (dma((groups,)),) * 2
     outs = pl.pallas_call(
@@ -534,7 +551,8 @@
             narrow, narrow, narrow, narrow, single, single,
             pltpu.VMEM((2,) + key_valid.shape, jnp.int32),
             pltpu.VMEM((4, rows, wide), F32),
-            scored, scored, stats, stats, stats,
+            scored, scored, stats, stats,
+            pltpu.VMEM((2, 8, rows), F32), bits, bits,
             pltpu.VMEM((3, rows, cols), F32),
             pltpu.VMEM((3, rows, cols), BF16), pltpu.VMEM((3, rows, cols), BF16),
             pltpu.VMEM((2, rows, cols), F32),

time: 45.1 us -> 44.8 us (level)
  no operation moved by 1% of the time
where the time goes in v6:
time: 44.8 us; the launch traced here: 44.6 us
  Pallas kernels  44 us (98%)
  between operations  0.64 us (1%)
    pallas_call x1, Pallas kernels, paired(): pl.pallas_call(functools.partial(fused_kernel, blks, rows, cols), out_sha...  42.7 us
    pallas_call x1, Pallas kernels, paired(): pl.pallas_call(copy_kernel, out_shape=(full,) * 7, in_specs=[pl.BlockSpec...  1.28 us

profile of v6, /device:TPU:0, one launch (start us, length us, event | category | flops | bytes accessed | tf_op | source)
XLA Modules:
  0.0 44.6 jit_solution(11334385577495785319)
XLA Ops:
  0.6 42.7 %attend_pairs.1 = (bf16[128,1024]{1,0:T(8,128)(2,1)S(1)}, bf16[128,1024]{1,0:T(8,128)(2,1)S(1)}, bf16[128,1024]{1,0:T(8,128)(2,1)S(1)}, bf16[128,1024]{1,0:T(8,1...) custom-call(s32[2,8]{1,0:T(2,128)} %offsets_ref.1, ...), custom_call_target="tpu_custom_call" | custom-call | tf_op jit(solution)/shard_map/attend_pairs/pallas_call | solution.py:543
  43.4 1.3 %hand_over.1 = (bf16[128,1024]{1,0:T(8,128)(2,1)}, bf16[128,1024]{1,0:T(8,128)(2,1)}, bf16[128,1024]{1,0:T(8,128)(2,1)}, bf16[128,1024]{1,0:T(8,128)(2,1)}, bf16...) custom-call(bf16[128,1024]{1,0:T(8,128)(2,1)S(1)} %get-tuple-element.21.refs_0_, ...), custom_call_target="tpu_custom_call" | custom-call | tf_op jit(solution)/shard_map/hand_over/pallas_call | solution.py:569

commit v7 on v6

--- a/solution.py
+++ b/solution.py
@@ -138,6 +138,9 @@
         pltpu.make_async_copy(cq_ref, side.at[1, 0], local_sem.at[4]),
         pltpu.make_async_copy(g_ref, side.at[2, 0], local_sem.at[5]),
     ]
+    meet(has_ahead, has_behind)
+    first = min(AHEAD, groups)
+    issue(0)
     for copy in locals_:
         copy.start()
     for chain, ref in enumerate((ck_ref, cv_ref)):
@@ -145,20 +148,6 @@
         def _():
             pltpu.make_async_copy(ref, mate, local_sem.at[6]).start()
 
-    @pl.when(jnp.logical_not(has_behind))
-    def _():
-        halo[...] = jnp.zeros(halo.shape, BF16)
-        far[...] = jnp.zeros(far.shape, BF16)
-        mask_ext[1] = jnp.zeros(mask_ext.shape[1:], jnp.int32)
-
-    @pl.when(jnp.logical_not(has_ahead))
-    def _():
-        x_recv[...] = jnp.zeros(x_recv.shape, BF16)
-        gfar[...] = jnp.zeros(gfar.shape, BF16)
-
-    meet(has_ahead, has_behind)
-    first = min(AHEAD, groups)
-    issue(0)
 
     @pl.when(has_ahead)
     def _():
@@ -170,6 +159,18 @@
         issue(g)
     for g in range(min(2, groups)):
         issue_halo(g)
+
+    @pl.when(jnp.logical_not(has_behind))
+    def _():
+        halo[...] = jnp.zeros(halo.shape, BF16)
+        far[...] = jnp.zeros(far.shape, BF16)
+        mask_ext[1] = jnp.zeros(mask_ext.shape[1:], jnp.int32)
+
+    @pl.when(jnp.logical_not(has_ahead))
+    def _():
+        x_recv[...] = jnp.zeros(x_recv.shape, BF16)
+        gfar[...] = jnp.zeros(gfar.shape, BF16)
+
     for copy in locals_:
         copy.wait()
     for chain, ref in enumerate((ck_ref, cv_ref)):

time: 44.8 us -> 44.8 us (level)
  no operation moved by 1% of the time
where the time goes in v7:
time: 44.8 us; the launch traced here: 44.6 us
  Pallas kernels  44 us (98%)
  between operations  0.64 us (1%)
    pallas_call x1, Pallas kernels, paired(): pl.pallas_call(functools.partial(fused_kernel, blks, rows, cols), out_sha...  42.7 us
    pallas_call x1, Pallas kernels, paired(): pl.pallas_call(copy_kernel, out_shape=(full,) * 7, in_specs=[pl.BlockSpec...  1.28 us

profile of v7, /device:TPU:0, one launch (start us, length us, event | category | flops | bytes accessed | tf_op | source)
XLA Modules:
  0.0 44.6 jit_solution(8643470063578107473)
XLA Ops:
  0.6 42.7 %attend_pairs.1 = (bf16[128,1024]{1,0:T(8,128)(2,1)S(1)}, bf16[128,1024]{1,0:T(8,128)(2,1)S(1)}, bf16[128,1024]{1,0:T(8,128)(2,1)S(1)}, bf16[128,1024]{1,0:T(8,1...) custom-call(s32[2,8]{1,0:T(2,128)} %offsets_ref.1, ...), custom_call_target="tpu_custom_call" | custom-call | tf_op jit(solution)/shard_map/attend_pairs/pallas_call | solution.py:544
  43.4 1.3 %hand_over.1 = (bf16[128,1024]{1,0:T(8,128)(2,1)}, bf16[128,1024]{1,0:T(8,128)(2,1)}, bf16[128,1024]{1,0:T(8,128)(2,1)}, bf16[128,1024]{1,0:T(8,128)(2,1)}, bf16...) custom-call(bf16[128,1024]{1,0:T(8,128)(2,1)S(1)} %get-tuple-element.21.refs_0_, ...), custom_call_target="tpu_custom_call" | custom-call | tf_op jit(solution)/shard_map/hand_over/pallas_call | solution.py:570

commit v8 on v6

--- a/solution.py
+++ b/solution.py
@@ -12,7 +12,7 @@
 WINDOW = 2048
 TILE = 512
 LAG = 4
-AHEAD = 5
+AHEAD = 4
 MESH = pl.DeviceIdType.MESH
 F32, BF16 = jnp.float32, jnp.bfloat16
 

time: 44.8 us -> 44.8 us (level)
  no operation moved by 1% of the time
where the time goes in v8:
time: 44.8 us; the launch traced here: 44.6 us
  Pallas kernels  44 us (98%)
  between operations  0.64 us (1%)
    pallas_call x1, Pallas kernels, paired(): pl.pallas_call(functools.partial(fused_kernel, blks, rows, cols), out_sha...  42.7 us
    pallas_call x1, Pallas kernels, paired(): pl.pallas_call(copy_kernel, out_shape=(full,) * 7, in_specs=[pl.BlockSpec...  1.28 us

profile of v8, /device:TPU:0, one launch (start us, length us, event | category | flops | bytes accessed | tf_op | source)
XLA Modules:
  0.0 44.6 jit_solution(11682493184524616274)
XLA Ops:
  0.6 42.7 %attend_pairs.1 = (bf16[128,1024]{1,0:T(8,128)(2,1)S(1)}, bf16[128,1024]{1,0:T(8,128)(2,1)S(1)}, bf16[128,1024]{1,0:T(8,128)(2,1)S(1)}, bf16[128,1024]{1,0:T(8,1...) custom-call(s32[2,8]{1,0:T(2,128)} %offsets_ref.1, ...), custom_call_target="tpu_custom_call" | custom-call | tf_op jit(solution)/shard_map/attend_pairs/pallas_call | solution.py:543
  43.4 1.3 %hand_over.1 = (bf16[128,1024]{1,0:T(8,128)(2,1)}, bf16[128,1024]{1,0:T(8,128)(2,1)}, bf16[128,1024]{1,0:T(8,128)(2,1)}, bf16[128,1024]{1,0:T(8,128)(2,1)}, bf16...) custom-call(bf16[128,1024]{1,0:T(8,128)(2,1)S(1)} %get-tuple-element.21.refs_0_, ...), custom_call_target="tpu_custom_call" | custom-call | tf_op jit(solution)/shard_map/hand_over/pallas_call | solution.py:569
